TPU v7x, 32 devices: a whole 2x2x4 slice. The times are simulated.
32 devices in a mesh: groups: 2 (over x), expert: 16 (over z, y, core).
Axes of the slice: x: 2, y: 2, z: 4, core: 2. Of those that a mesh axis runs over, the one named last changes fastest.
Arguments:
- routes: int32 [2, 2048, 8], P(None, ('groups', 'expert')), parts along dimension 1, may hold values from 0 to 31, as said below
- gate_weights: float32 [2, 2048, 8], P(None, ('groups', 'expert')), parts along dimension 1, may hold values from 0.05 to 0.5
- grad_out: bfloat16 [2, 2048, 2048], P(None, ('groups', 'expert')), parts along dimension 1, may hold values from -6 to 6
- saved_hidden: bfloat16 [4, 32, 384, 768], P('groups', 'expert'), parts along dimension 0, may hold values from -20 to 20
- down_weight: bfloat16 [32, 768, 2048], P('expert'), may hold values from -0.21875 to 0.21875
Outputs:
- hidden_grad: bfloat16 [2, 2048, 8, 768], P(None, ('groups', 'expert')), parts along dimension 1
- update: bfloat16 [32, 1536, 2048], P('expert', 'groups'), parts along dimension 1
There are 2 independent parts, one for each index of `groups`. A program takes and returns all parts, laid end to end along the dimension named above; an argument that names none is the same for every part. Nothing has to cross between parts.
Inputs may be any that keep to these rules, and one draw needn't show every extreme that they name: `routes`: each token names 8 different experts. In each micro-batch the 64 tokens of one source name any expert at most 24 times, and some expert exactly 24 times by the tokens of every source.
All inputs are finite; a program needn't handle non-finite values.
Results may differ from a plain program's by a relative error of at most 0.011.
Values may be sent and summed in bfloat16 or wider, within the bound.
No kernel may reach another device: no remote copies, remote signals or barrier semaphores. Data moves between devices by JAX's collectives and lax.ppermute only.
A program may use at most 128 MiB of HBM per device.

v0:
```python
import math

import jax
import jax.numpy as jnp
from jax import lax
from jax.sharding import PartitionSpec as P

COEF_A = 3.4445
COEF_B = -4.775
COEF_C = 2.0315


def pick_rows(source_table, row_index):
    return jnp.take(source_table, row_index, axis=0)


def row_places(routes, capacity, experts):
    matches = (routes[..., None] == jnp.arange(experts, dtype=jnp.int32)).astype(jnp.int32)
    per_token = jnp.sum(matches, axis=2)
    earlier = jnp.cumsum(per_token, axis=1) - per_token
    slot_index = jnp.sum(matches * earlier[:, :, None, :], axis=3)
    return routes * capacity + slot_index


def fill_slots(places, gate_weights, grad_out, slot_total):
    batches, tokens, top_count = places.shape
    flat_place = places.reshape(batches, 1, tokens * top_count)
    target = jnp.arange(slot_total, dtype=jnp.int32)[None, :, None]
    matched = flat_place == target
    token_ids = (jnp.arange(tokens * top_count, dtype=jnp.int32) // top_count)[None, None, :]
    source_token = jnp.sum(jnp.where(matched, token_ids, 0), axis=2)
    slot_gate = jnp.sum(
        jnp.where(matched, gate_weights.reshape(batches, 1, tokens * top_count), 0.0), axis=2
    )
    picked_rows = jax.vmap(pick_rows)(grad_out, source_token)
    return (slot_gate[:, :, None] * picked_rows.astype(jnp.float32)).astype(jnp.bfloat16)


def orthogonal_step(weight_grad, model_width):
    hidden_width = weight_grad.shape[1]
    gram_raw = jnp.einsum(
        "efd,egd->efg", weight_grad, weight_grad, preferred_element_type=jnp.float32
    )
    frob_norm = jnp.sqrt(jnp.sum(gram_raw * gram_raw, axis=(1, 2))) + 1e-06
    gram_unit = gram_raw / frob_norm[:, None, None]
    gram_half = gram_unit.astype(jnp.bfloat16)
    identity = jnp.eye(hidden_width, dtype=jnp.float32)[None]
    square_first = jnp.einsum(
        "efg,egh->efh", gram_half, gram_half, preferred_element_type=jnp.float32
    )
    poly_first = (COEF_A * identity + COEF_B * gram_unit + COEF_C * square_first).astype(
        jnp.bfloat16
    )
    left_product = jnp.einsum(
        "efg,egh->efh", poly_first, gram_half, preferred_element_type=jnp.float32
    ).astype(jnp.bfloat16)
    gram_next = jnp.einsum(
        "efg,egh->efh", left_product, poly_first, preferred_element_type=jnp.float32
    )
    next_half = gram_next.astype(jnp.bfloat16)
    square_next = jnp.einsum(
        "efg,egh->efh", next_half, next_half, preferred_element_type=jnp.float32
    )
    poly_next = (COEF_A * identity + COEF_B * gram_next + COEF_C * square_next).astype(jnp.bfloat16)
    product = jnp.einsum("efg,egh->efh", poly_next, poly_first, preferred_element_type=jnp.float32)
    scaling = math.sqrt(model_width) / jnp.sqrt(frob_norm)
    combined = (product * scaling[:, None, None]).astype(jnp.bfloat16)
    return jnp.einsum(
        "efg,egd->efd", combined, weight_grad, preferred_element_type=jnp.float32
    ).astype(jnp.bfloat16)


def local(routes, gate_weights, grad_out, saved_hidden, down_weight):
    devices = lax.axis_size("expert")
    local_experts = down_weight.shape[0]
    hidden_width = down_weight.shape[1]
    model_width = down_weight.shape[2]
    experts = devices * local_experts
    batches = saved_hidden.shape[0]
    slot_count = saved_hidden.shape[2]
    capacity = slot_count // devices
    tokens = routes.shape[1]
    top_count = routes.shape[2]
    places = row_places(routes, capacity, experts)
    outgoing = fill_slots(places, gate_weights, grad_out, experts * capacity)
    outgoing = outgoing.reshape(batches, devices, local_experts, capacity, model_width)
    arrived = lax.all_to_all(outgoing, "expert", split_axis=1, concat_axis=3, tiled=True)
    received = arrived.reshape(batches, local_experts, slot_count, model_width)
    slot_grad = jnp.einsum(
        "mjsd,jfd->mjsf", received, down_weight, preferred_element_type=jnp.float32
    ).astype(jnp.bfloat16)
    returned = lax.all_to_all(
        slot_grad.reshape(batches, 1, local_experts, slot_count, hidden_width),
        "expert",
        split_axis=3,
        concat_axis=1,
        tiled=True,
    )
    back_table = returned.reshape(batches, experts * capacity, hidden_width)
    hidden_grad = jax.vmap(pick_rows)(back_table, places.reshape(batches, tokens * top_count))
    hidden_grad = hidden_grad.reshape(batches, tokens, top_count, hidden_width)
    weight_grad = jnp.einsum(
        "mjsf,mjsd->jfd", saved_hidden, received, preferred_element_type=jnp.float32
    ).astype(jnp.bfloat16)
    update = orthogonal_step(weight_grad, model_width)
    return (hidden_grad, update)


def solution(mesh):
    in_specs = (
        P(None, ("groups", "expert"), None),
        P(None, ("groups", "expert"), None),
        P(None, ("groups", "expert"), None),
        P("groups", "expert", None, None),
        P("expert", None, None),
    )
    out_specs = (P(None, ("groups", "expert"), None, None), P("expert", "groups", None))
    return jax.shard_map(local, mesh=mesh, in_specs=in_specs, out_specs=out_specs, check_vma=False)
```

profile of v0, /device:TPU:15, one launch (start us, length us, event | category | flops | bytes accessed | tf_op | source)
XLA Modules:
  0.0 294.3 jit_solution(15632452333136307427)
XLA Ops:
  0.7 0.9 convert_reduce_fusion
  1.7 0.1 reduce_window_sum.11
  1.8 0.8 select_reduce_fusion.2
  2.6 0.7 compare_and_fusion.1
  3.4 0.1 reshape.126
  3.5 0.4 select_reduce_fusion
  4.0 0.1 reduce_sum.53
  4.2 0.8 copy.45
  5.0 0.1 broadcast_in_dim.56
  5.1 0.4 select_reduce_fusion.1
  5.5 0.1 mul.60
  5.7 33.1 %gather_fusion = bf16[1536,2048]{1,0:T(8,128)(2,1)} fusion(bf16[2,64,2048]{2,1,0:T(8,128)(2,1)S(1)} %copy-done.2, s32[1536]{0:T(1024)S(1)} %reshape.131), kind=kCustom, calls=%fused_computation | custom fusion | bytes 12595200 | tf_op jit(solution)/shard_map/vmap(jit(_take))/gather | solution.py:14
  38.8 7.2 %multiply_convert_fusion = bf16[2,16,2,24,2048]{4,3,0,2,1:T(8,128)(2,1)} fusion(bf16[2,16,2,24,2048]{4,3,2,1,0:T(8,128)(2,1)} %bitcast.42, f32[2,16,2,24]{3,0,2,1:T(2,128)S(1)} %copy.46, pred[2,16,2,24]{3,0,2,1:T(4,128)(4,1)S(1)} %copy.47), kind=kLoop, calls=%fused_computation.3 | loop fusion | flops 12582912 | bytes 12590592 | tf_op jit(solution)/shard_map/convert_element_type | solution.py:36
  45.9 6.5 %all-to-all-start = ((bf16[2,16,2,24,2048]{4,3,0,2,1:T(8,128)(2,1)}), bf16[2,16,2,24,2048]{4,3,0,2,1:T(8,128)(2,1)}, u32[]{:S(2)}, u32[]{:S(2)}) async-start(bf16[2,16,2,24,2048]{4,3,0,2,1:T(8,128)(2,1)} %multiply_convert_fusion), calls=%async_computation | async-start | bytes 12582912 | tf_op jit(solution)/shard_map/all_to_all | solution.py:87
  52.6 0.1 copy.43
  52.7 1.5 fusion.12
  54.3 135.6 %all-to-all-done = bf16[2,16,2,24,2048]{4,3,0,2,1:T(8,128)(2,1)} async-done(((bf16[2,16,2,24,2048]{4,3,0,2,1:T(8,128)(2,1)}), bf16[2,16,2,24,2048]{4,3,0,2,1:T(8,128)(2,1)}, u32[]{:S(2)}, u32[]{:S(2)}) %all-to-all-start) | async-done | bytes 6291488 | tf_op jit(solution)/shard_map/all_to_all | solution.py:87
  189.9 3.4 %copy.49 = bf16[2,1,2,16,24,2048]{5,4,3,0,2,1:T(8,128)(2,1)S(1)} copy(bf16[2,1,2,16,24,2048]{5,4,0,2,3,1:T(8,128)(2,1)} %bitcast.3) | data formatting | bytes 12582912 | tf_op jit(solution)/shard_map/all_to_all | solution.py:87
  193.2 8.1 %convert_bitcast_fusion = bf16[2,1,2,384,768]{4,3,0,2,1:T(8,128)(2,1)S(1)} fusion(bf16[2,2,384,2048]{3,2,0,1:T(8,128)(2,1)S(1)} %bitcast.44, bf16[2,768,2048]{2,1,0:T(8,128)(2,1)} %param.9), kind=kOutput, calls=%fused_computation.27 | convolution fusion | flops 4833017856 | bytes 14942208 | tf_op jit(solution)/shard_map/mjsd,jfd->mjsf/dot_general | solution.py:89
  201.4 7.3 %bitcast_convert_fusion = bf16[2,2048,768]{2,1,0:T(8,128)(2,1)} fusion(bf16[2,2,384,2048]{3,2,0,1:T(8,128)(2,1)S(1)} %bitcast.45, bf16[2,2,384,768]{3,2,1,0:T(8,128)(2,1)S(1)} %copy-done), kind=kOutput, calls=%fused_computation.2 | convolution fusion | flops 4834983936 | bytes 14942208 | tf_op jit(solution)/shard_map/mjsf,mjsd->jfd/dot_general | solution.py:102
  208.7 3.8 %copy.50 = bf16[2,1,2,384,768]{4,0,2,1,3:T(2,128)(2,1)} copy(bf16[2,1,2,384,768]{4,3,0,2,1:T(8,128)(2,1)S(1)} %convert_bitcast_fusion) | data formatting | bytes 4718592 | tf_op jit(solution)/shard_map/reshape | solution.py:93
  212.5 4.8 %all-to-all-start.1 = ((bf16[2,1,2,384,768]{4,0,2,1,3:T(2,128)(2,1)}), bf16[2,1,2,384,768]{4,0,2,1,3:T(2,128)(2,1)S(1)}, u32[]{:S(2)}, u32[]{:S(2)}) async-start(bf16[2,1,2,384,768]{4,0,2,1,3:T(2,128)(2,1)} %copy.50), calls=%async_computation.1 | async-start | bytes 4718592 | tf_op jit(solution)/shard_map/all_to_all | solution.py:92
  217.3 9.5 %multiply_reduce_fusion = (f32[2]{0:T(128)S(1)}, f32[2,768,768]{2,1,0:T(8,128)S(1)}) fusion(bf16[2,2048,768]{2,1,0:T(8,128)(2,1)} %bitcast_convert_fusion), kind=kOutput, calls=%fused_computation.10 | convolution fusion | flops 4834197504 | bytes 11010056 | tf_op jit(solution)/shard_map/efd,egd->efg/dot_general | solution.py:41
  226.8 2.2 copy-done.4
  228.9 3.8 %add_convert_fusion.1 = bf16[2,768,768]{2,1,0:T(8,128)(2,1)} fusion(f32[768,768]{1,0:T(8,128)S(1)} %copy-done.3, f32[2,768,768]{2,1,0:T(8,128)S(1)} %get-tuple-element.7, f32[2]{0:T(128)S(1)} %get-tuple-element.5), kind=kOutput, calls=%fused_computation.9 | convolution fusion | flops 1821376512 | bytes 9437192 | tf_op jit(solution)/shard_map/efg,egh->efh/dot_general | solution.py:48
  232.7 9.9 %fusion.7 = f32[2,768,768]{2,1,0:T(8,128)} fusion(bf16[2,768,768]{2,1,0:T(8,128)(2,1)} %add_convert_fusion.1, f32[2,768,768]{2,1,0:T(8,128)} %copy-done.4, f32[2]{0:T(128)S(1)} %get-tuple-element.5), kind=kOutput, calls=%fused_computation.20 | convolution fusion | flops 3627417600 | bytes 11796488 | tf_op jit(solution)/shard_map/efg,egh->efh/dot_general | solution.py:57
  242.6 13.0 %fusion.2 = f32[2,768,768]{2,1,0:T(8,128)} fusion(bf16[2,768,768]{2,1,0:T(8,128)(2,1)} %add_convert_fusion.1, f32[2,768,768]{2,1,0:T(8,128)} %fusion.7, f32[768,768]{1,0:T(8,128)} %fusion.12), kind=kOutput, calls=%fused_computation.15 | convolution fusion | flops 3630956544 | bytes 14155776 | tf_op jit(solution)/shard_map/efg,egh->efh/dot_general | solution.py:65
  255.6 10.3 %convolution_convert_fusion = bf16[2,768,2048]{2,1,0:T(8,128)(2,1)} fusion(bf16[2,2048,768]{2,1,0:T(8,128)(2,1)} %bitcast_convert_fusion, f32[2,768,768]{2,1,0:T(8,128)} %fusion.2, f32[2]{0:T(128)S(1)} %get-tuple-element.4), kind=kOutput, calls=%fused_computation.11 | convolution fusion | flops 4837343232 | bytes 17301512 | tf_op jit(solution)/shard_map/efg,egd->efd/dot_general | solution.py:68
  265.9 4.4 %all-to-all-done.1 = bf16[2,1,2,384,768]{4,0,2,1,3:T(2,128)(2,1)S(1)} async-done(((bf16[2,1,2,384,768]{4,0,2,1,3:T(2,128)(2,1)}), bf16[2,1,2,384,768]{4,0,2,1,3:T(2,128)(2,1)S(1)}, u32[]{:S(2)}, u32[]{:S(2)}) %all-to-all-start.1) | async-done | bytes 2359328 | tf_op jit(solution)/shard_map/all_to_all | solution.py:92
  270.3 1.7 copy.51
  272.0 19.5 %gather_fusion.1 = bf16[1024,768]{1,0:T(8,128)(2,1)} fusion(bf16[2,768,768]{2,1,0:T(8,128)(2,1)} %bitcast.40, s32[1024]{0:T(1024)S(1)} %bitcast.41), kind=kCustom, calls=%fused_computation.1 | custom fusion | bytes 3153920 | tf_op jit(solution)/shard_map/vmap(jit(_take))/gather | solution.py:14
  291.5 2.8 broadcast_select_fusion
  (23 shorter events, 0.5 us)
Async XLA Ops:
  0.6 200.7 %copy-start = (bf16[2,2,384,768]{3,2,1,0:T(8,128)(2,1)S(1)}, bf16[2,2,384,768]{3,2,1,0:T(8,128)(2,1)}, u32[]{:S(2)}) copy-start(bf16[2,2,384,768]{3,2,1,0:T(8,128)(2,1)} %param.8) | copy-start | bytes 7077892
  0.6 5.0 %copy-start.2 = (bf16[2,64,2048]{2,1,0:T(8,128)(2,1)S(1)}, bf16[2,64,2048]{2,1,0:T(8,128)(2,1)}, u32[]{:S(2)}) copy-start(bf16[2,64,2048]{2,1,0:T(8,128)(2,1)} %param.7) | copy-start | bytes 1572868
  45.9 143.9 %all-to-all-start = ((bf16[2,16,2,24,2048]{4,3,0,2,1:T(8,128)(2,1)}), bf16[2,16,2,24,2048]{4,3,0,2,1:T(8,128)(2,1)}, u32[]{:S(2)}, u32[]{:S(2)}) async-start(bf16[2,16,2,24,2048]{4,3,0,2,1:T(8,128)(2,1)} %multiply_convert_fusion), calls=%async_computation | async-start | bytes 12582912 | tf_op jit(solution)/shard_map/all_to_all | solution.py:87
  212.5 57.8 %all-to-all-start.1 = ((bf16[2,1,2,384,768]{4,0,2,1,3:T(2,128)(2,1)}), bf16[2,1,2,384,768]{4,0,2,1,3:T(2,128)(2,1)S(1)}, u32[]{:S(2)}, u32[]{:S(2)}) async-start(bf16[2,1,2,384,768]{4,0,2,1,3:T(2,128)(2,1)} %copy.50), calls=%async_computation.1 | async-start | bytes 4718592 | tf_op jit(solution)/shard_map/all_to_all | solution.py:92
  217.3 11.7 %copy-start.3 = (f32[768,768]{1,0:T(8,128)S(1)}, f32[768,768]{1,0:T(8,128)}, u32[]{:S(2)}) copy-start(f32[768,768]{1,0:T(8,128)} %fusion.12) | copy-start | bytes 7077892
  226.7 2.2 copy-start.4
  272.0 22.2 %copy-start.1 = (bf16[2,2,384,768]{3,2,1,0:T(8,128)(2,1)S(1)}, bf16[2,2,384,768]{3,2,1,0:T(8,128)(2,1)}, u32[]{:S(2)}) copy-start(bf16[2,2,384,768]{3,2,1,0:T(8,128)(2,1)} %param.8) | copy-start | bytes 7077892
where the time goes:
time: 295 us; the launch traced here: 294 us
  waiting for transfers between devices  140 us (47%)
  local copies, waits for them, and re-layouts  65.4 us (22%)
  matrix products  61.9 us (21%)
  other arithmetic  14.9 us (5%)
  starting transfers between devices  11.3 us (4%)
    all_to_all x1, waiting for transfers between devices, local(): lax.all_to_all(outgoing, 'expert', split_axis=1, concat_axis=3, tiled=True)  136 us
    gather x3, local copies, waits for them, and re-layouts, pick_rows(): return jnp.take(source_table, row_index, axis=0)  52.6 us
    dot_general x1, matrix products, orthogonal_step(): jnp.einsum('efg,egh->efh', poly_next, poly_first, preferred_element_type=...  13 us
    dot_general x1, matrix products, orthogonal_step(): jnp.einsum('efg,egd->efd', combined, weight_grad, preferred_element_type=...  10.3 us
    dot_general x1, matrix products, orthogonal_step(): jnp.einsum('efg,egh->efh', left_product, poly_first, preferred_element_ty...  9.89 us
    dot_general x1, matrix products, orthogonal_step(): jnp.einsum('efd,egd->efg', weight_grad, weight_grad, preferred_element_ty...  9.48 us
    dot_general x1, matrix products, local(): jnp.einsum('mjsd,jfd->mjsf', received, down_weight, preferred_element_typ...  8.13 us
    dot_general x1, matrix products, local(): jnp.einsum('mjsf,mjsd->jfd', saved_hidden, received, preferred_element_ty...  7.3 us
  transfers between devices with their start and end apart: 2, of which 2 were waited for; matrix products, arithmetic and copies ran while one was open for 16% of the time, Pallas kernels for 0%

commit v1 on v0

v1 whole, which is shorter than its diff:
```python
import functools
import math

import jax
import jax.numpy as jnp
import numpy as np
from jax import lax
from jax.experimental import pallas as pl
from jax.experimental.pallas import tpu as pltpu
from jax.sharding import PartitionSpec as P

COEF_A = 3.4445
COEF_B = -4.775
COEF_C = 2.0315
AXIS = "expert"
NT = (((1,), (1,)), ((), ()))


def ring_layout(mesh):
    row = np.asarray(mesh.devices)[0].reshape(-1)
    chips = len(row) // 2
    coords = [getattr(d, "coords", None) for d in row[::2]]
    if any(c is None for c in coords):
        return list(range(chips))
    ys = sorted({c[1] for c in coords})
    if len(ys) != 2:
        return list(range(chips))
    first = [i for i in range(chips) if coords[i][1] == ys[0]]
    second = [i for i in range(chips) if coords[i][1] == ys[1]]
    first.sort(key=lambda i: coords[i][2])
    second.sort(key=lambda i: -coords[i][2])
    return first + second


def shift_pairs(order, step):
    chips = len(order)
    return [
        (order[p] * 2 + core, order[(p + step) % chips] * 2 + core)
        for p in range(chips)
        for core in range(2)
    ]


def swap_pairs(devices):
    return [(i, i ^ 1) for i in range(devices)]


def source_table(order):
    chips = len(order)
    place = {chip: p for p, chip in enumerate(order)}
    table = np.zeros((chips * 2, chips * 2), np.int32)
    for i in range(chips * 2):
        p, core = place[i // 2], i % 2
        steps = [0]
        for s in range(1, chips // 2):
            steps += [-s, s]
        steps.append(chips // 2)
        row = []
        for s in steps:
            chip = order[(p + s) % chips]
            row += [chip * 2 + core, chip * 2 + 1 - core]
        table[i] = row
    return table


def spread_small(value, devices):
    gathered = value[None]
    bit = 1
    while bit < devices:
        other = lax.ppermute(gathered, AXIS, [(i, i ^ bit) for i in range(devices)])
        gathered = jnp.concatenate([gathered, other], axis=0)
        bit *= 2
    return gathered


def expert_kernel(count, first, ids_ref, me_ref, *refs):
    tok_refs = refs[: 2 * count]
    refs = refs[2 * count :]
    if first:
        sel_hbm, gate_hbm, w_hbm, disp_out, grad_out = refs[:5]
        refs = refs[5:]
    else:
        sel_hbm, gate_hbm, w_hbm, _, _, disp_out, grad_out = refs[:7]
        refs = refs[7:]
    tok, sel, gate, w, rows, back, in_sem, w_sem, out_sem = refs
    width = tok.shape[2]
    half = tok.shape[1] // 2
    part = rows.shape[1] // count
    hidden = w.shape[1]
    sources = [ids_ref[i] for i in range(count)]
    slots = [jnp.bitwise_xor(me_ref[0], s) for s in sources]
    loads = []
    for i in range(count):
        loads.append(
            [
                pltpu.make_async_copy(tok_refs[2 * i], tok.at[i, pl.ds(0, half)], in_sem.at[i, 0]),
                pltpu.make_async_copy(tok_refs[2 * i + 1], tok.at[i, pl.ds(half, half)], in_sem.at[i, 1]),
                pltpu.make_async_copy(sel_hbm.at[slots[i]], sel.at[i], in_sem.at[i, 2]),
                pltpu.make_async_copy(gate_hbm.at[slots[i]], gate.at[i], in_sem.at[i, 3]),
            ]
        )
        for c in loads[i]:
            c.start()
    w_loads = [pltpu.make_async_copy(w_hbm.at[e], w.at[e], w_sem.at[e]) for e in range(2)]
    for c in w_loads:
        c.start()
    stores = []
    step = min(512, width)
    for i in range(count):
        for c in loads[i]:
            c.wait()
        for at in range(0, width, step):
            picked = jnp.dot(sel[i], tok[i, :, at : at + step], preferred_element_type=jnp.float32)
            gated = (picked * gate[i]).astype(jnp.bfloat16)
            for e in range(2):
                rows[e, i * part : (i + 1) * part, at : at + step] = gated[e * part : (e + 1) * part]
        for e in range(2):
            c = pltpu.make_async_copy(
                rows.at[e, pl.ds(i * part, part)], disp_out.at[e, sources[i]], out_sem.at[i, e]
            )
            c.start()
            stores.append(c)
    for e in range(2):
        w_loads[e].wait()
        for at in range(0, hidden, 256):
            product = lax.dot_general(
                rows[e], w[e, at : at + 256, :], NT, preferred_element_type=jnp.float32
            ).astype(jnp.bfloat16)
            for i in range(count):
                back[i, e, :, at : at + 256] = product[i * part : (i + 1) * part]
    for i in range(count):
        c = pltpu.make_async_copy(back.at[i], grad_out.at[sources[i]], out_sem.at[i, 2])
        c.start()
        stores.append(c)
    for c in stores:
        c.wait()


def expert_rows(ids, me, chunks, sel, gate, weight, carried):
    devices, part2, tokens = sel.shape
    part = part2 // 2
    hidden, width = weight.shape[1:]
    count = len(chunks)
    operands = []
    for pair in chunks:
        operands += list(pair)
    any_spec = pl.BlockSpec(memory_space=pl.ANY)
    smem = pl.BlockSpec(memory_space=pltpu.SMEM)
    first = carried is None
    args = [ids, me, *operands, sel, gate, weight]
    aliases = {}
    if not first:
        aliases = {len(args): 0, len(args) + 1: 1}
        args += list(carried)
    flops = 2 * count * part2 * (tokens * width + width * hidden)
    moved = weight.size * 2 + count * (tokens * width + part2 * (width + hidden)) * 2
    return pl.pallas_call(
        functools.partial(expert_kernel, count, first),
        out_shape=(
            jax.ShapeDtypeStruct((2, devices, part, width), jnp.bfloat16),
            jax.ShapeDtypeStruct((devices, 2, part, hidden), jnp.bfloat16),
        ),
        in_specs=[smem, smem] + [any_spec] * (len(args) - 2),
        out_specs=(any_spec, any_spec),
        scratch_shapes=[
            pltpu.VMEM((count, tokens, width), jnp.bfloat16),
            pltpu.VMEM((count, part2, tokens), jnp.bfloat16),
            pltpu.VMEM((count, part2, 1), jnp.float32),
            pltpu.VMEM((2, hidden, width), jnp.bfloat16),
            pltpu.VMEM((2, count * part, width), jnp.bfloat16),
            pltpu.VMEM((count, 2, part, hidden), jnp.bfloat16),
            pltpu.SemaphoreType.DMA((count, 4)),
            pltpu.SemaphoreType.DMA((2,)),
            pltpu.SemaphoreType.DMA((count, 3)),
        ],
        input_output_aliases=aliases,
        cost_estimate=pl.CostEstimate(flops=flops, bytes_accessed=moved, transcendentals=0),
        compiler_params=pltpu.CompilerParams(vmem_limit_bytes=40 << 20),
        name=f"expert_rows_{count}",
    )(*args)


def slot_tables(small, me, capacity):
    routes, gates = small[:, 0], small[:, 1]
    devices, batches, top, tokens = routes.shape
    mine = (2 * me + jnp.arange(2)).astype(jnp.float32)
    hit = routes[:, None] == mine[None, :, None, None, None]
    named = jnp.sum(hit.astype(jnp.float32), axis=3)
    gate = jnp.sum(jnp.where(hit, gates[:, None], 0.0), axis=3)
    before = jnp.triu(jnp.ones((tokens, tokens), jnp.float32), 1)
    rank = jnp.einsum("deba,at->debt", named, before)
    slot = jnp.arange(capacity, dtype=jnp.float32)[:, None]
    pick = (rank[:, :, :, None, :] == slot) & (named[:, :, :, None, :] > 0.5)
    row_gate = jnp.sum(jnp.where(pick, gate[:, :, :, None, :], 0.0), axis=4)
    same = jnp.eye(batches, dtype=bool)[None, None, :, None, :, None]
    wide = pick[:, :, :, :, None, :] & same
    rows = 2 * batches * capacity
    return (
        wide.astype(jnp.bfloat16).reshape(devices, rows, batches * tokens),
        row_gate.reshape(devices, rows, 1),
    )


def own_places(routes, experts, capacity):
    matches = (routes[..., None] == jnp.arange(experts, dtype=jnp.int32)).astype(jnp.int32)
    per_token = jnp.sum(matches, axis=2)
    earlier = jnp.cumsum(per_token, axis=1) - per_token
    slot = jnp.sum(matches * earlier[:, :, None, :], axis=3)
    batches = routes.shape[0]
    batch = jnp.arange(batches, dtype=jnp.int32)[:, None, None]
    return (routes * batches + batch) * capacity + slot


def orthogonal_step(weight_grad, model_width):
    hidden_width = weight_grad.shape[1]
    gram_raw = jnp.einsum("efd,egd->efg", weight_grad, weight_grad, preferred_element_type=jnp.float32)
    frob_norm = jnp.sqrt(jnp.sum(gram_raw * gram_raw, axis=(1, 2))) + 1e-06
    gram_unit = gram_raw / frob_norm[:, None, None]
    gram_half = gram_unit.astype(jnp.bfloat16)
    identity = jnp.eye(hidden_width, dtype=jnp.float32)[None]

    def product(a, b):
        return jnp.einsum("efg,egh->efh", a, b, preferred_element_type=jnp.float32)

    square_first = product(gram_half, gram_half)
    poly_first = (COEF_A * identity + COEF_B * gram_unit + COEF_C * square_first).astype(jnp.bfloat16)
    left_product = product(poly_first, gram_half).astype(jnp.bfloat16)
    gram_next = product(left_product, poly_first)
    next_half = gram_next.astype(jnp.bfloat16)
    square_next = product(next_half, next_half)
    poly_next = (COEF_A * identity + COEF_B * gram_next + COEF_C * square_next).astype(jnp.bfloat16)
    scaling = math.sqrt(model_width) / jnp.sqrt(frob_norm)
    combined = (product(poly_next, poly_first) * scaling[:, None, None]).astype(jnp.bfloat16)
    return jnp.einsum("efg,egd->efd", combined, weight_grad, preferred_element_type=jnp.float32).astype(
        jnp.bfloat16
    )


def local(order, routes, gate_weights, grad_out, saved_hidden, down_weight):
    devices = lax.axis_size(AXIS)
    me = lax.axis_index(AXIS)
    chips = devices // 2
    local_experts, hidden, width = down_weight.shape
    batches, tokens, top = routes.shape
    slots = saved_hidden.shape[2]
    capacity = slots // devices
    experts = devices * local_experts
    ahead, behind, swap = shift_pairs(order, 1), shift_pairs(order, -1), swap_pairs(devices)

    def swapped(x):
        return lax.ppermute(x, AXIS, swap)

    small = jnp.stack(
        [jnp.swapaxes(routes, 1, 2).astype(jnp.float32), jnp.swapaxes(gate_weights, 1, 2)]
    )
    groups = [[grad_out]]
    right = left = grad_out
    for step in range(1, chips // 2):
        right = lax.ppermute(right, AXIS, ahead)
        left = lax.ppermute(left, AXIS, behind)
        groups.append([right, left])
    last = (lax.ppermute(right[0], AXIS, ahead), lax.ppermute(left[1], AXIS, behind))
    small = spread_small(small, devices)
    sel, gate = slot_tables(small, me, capacity)
    ids = jnp.asarray(source_table(order))[me]
    me1 = me.reshape(1).astype(jnp.int32)

    carried = None
    done = 0
    for group in groups:
        chunks = []
        for x in group:
            other = swapped(x)
            chunks += [(x[0], x[1]), (other[0], other[1])]
        carried = expert_rows(ids[done : done + len(chunks)], me1, chunks, sel, gate, down_weight, carried)
        done += len(chunks)
    other = (swapped(last[0]), swapped(last[1]))
    carried = expert_rows(ids[done : done + 2], me1, [last, other], sel, gate, down_weight, carried)
    dispatched, slot_grad = carried

    returned = lax.all_to_all(slot_grad, AXIS, split_axis=0, concat_axis=0, tiled=True)

    hidden_rows = saved_hidden.reshape(batches, local_experts, devices, capacity, hidden)
    hidden_rows = jnp.transpose(hidden_rows, (1, 2, 0, 3, 4)).reshape(local_experts, -1, hidden)
    weight_grad = jnp.einsum(
        "jsf,jsd->jfd",
        hidden_rows,
        dispatched.reshape(local_experts, -1, width),
        preferred_element_type=jnp.float32,
    ).astype(jnp.bfloat16)
    update = orthogonal_step(weight_grad, width)

    places = own_places(routes, experts, capacity).reshape(-1, 1)
    table = returned.reshape(-1, hidden)
    chosen = (places == jnp.arange(table.shape[0], dtype=jnp.int32)[None]).astype(jnp.bfloat16)
    hidden_grad = jnp.dot(chosen, table, preferred_element_type=jnp.float32).astype(jnp.bfloat16)
    return hidden_grad.reshape(batches, tokens, top, hidden), update


def solution(mesh):
    in_specs = (
        P(None, ("groups", AXIS), None),
        P(None, ("groups", AXIS), None),
        P(None, ("groups", AXIS), None),
        P("groups", AXIS, None, None),
        P(AXIS, None, None),
    )
    out_specs = (P(None, ("groups", AXIS), None, None), P(AXIS, "groups", None))
    return jax.shard_map(
        functools.partial(local, ring_layout(mesh)),
        mesh=mesh,
        in_specs=in_specs,
        out_specs=out_specs,
        check_vma=False,
    )
```

time: 295 us -> 177 us (0.60)
  waiting for transfers between devices: 140 us -> 38.5 us
  local copies, waits for them, and re-layouts: 65.4 us -> 8.74 us
  Pallas kernels: 0 us -> 36.5 us
  starting transfers between devices: 11.3 us -> 23.7 us
  other arithmetic: 14.9 us -> 7.61 us
    all_to_all x2 -> x1, waiting for transfers between devices: 140 us -> 11.2 us  [local(): lax.all_to_all(slot_grad, AXIS, split_axis=0, concat_axis=0, tiled=True)]
    gather x3 -> x0, local copies, waits for them, and re-layouts: 52.6 us -> none  [pick_rows(): return jnp.take(source_table, row_index, axis=0)]
    pallas_call x0 -> x5, Pallas kernels: none -> 36.5 us  [expert_rows(): pl.pallas_call(functools.partial(expert_kernel, count, first), out_shape=...]
    ppermute x0 -> x21, waiting for transfers between devices: none -> 27.2 us  [the longest x3 11.1 us: local(): right = lax.ppermute(right, AXIS, ahead)]
    ppermute x0 -> x21, starting transfers between devices: none -> 18.1 us  [the longest x9 7.19 us: swapped(): return lax.ppermute(x, AXIS, swap)]
    convert_element_type x1 -> x2, other arithmetic: 7.16 us -> 0.11 us  [the longest x1 0.11 us: slot_tables(): wide.astype(jnp.bfloat16).reshape(devices, rows, batches * tokens)]
    all_to_all x2 -> x1, starting transfers between devices: 11.3 us -> 5.58 us  [local(): lax.all_to_all(slot_grad, AXIS, split_axis=0, concat_axis=0, tiled=True)]
    all_to_all x2 -> x0, local copies, waits for them, and re-layouts: 5.09 us -> none  [the longest x1 3.36 us: local(): lax.all_to_all(outgoing, 'expert', split_axis=1, concat_axis=3, tiled=True)]
  transfers between devices with their start and end apart: 2 -> 22, of which waited for: 2 -> 7; matrix products, arithmetic and copies ran while one was open for 16% -> 33% of each run, Pallas kernels for 0% -> 17%
where the time goes in v1:
time: 177 us
  matrix products  60.5 us (34%)
  waiting for transfers between devices  38.5 us (22%)
  Pallas kernels  36.5 us (21%)
  starting transfers between devices  23.7 us (13%)
  local copies, waits for them, and re-layouts  8.74 us (5%)
  other arithmetic  7.61 us (4%)
    pallas_call x5, Pallas kernels, expert_rows(): pl.pallas_call(functools.partial(expert_kernel, count, first), out_shape=...  36.5 us
    dot_general x3, matrix products, product(): return jnp.einsum('efg,egh->efh', a, b, preferred_element_type=jnp.float32)  31.6 us
    all_to_all x1, waiting for transfers between devices, local(): lax.all_to_all(slot_grad, AXIS, split_axis=0, concat_axis=0, tiled=True)  11.2 us
    ppermute x3, waiting for transfers between devices, local(): right = lax.ppermute(right, AXIS, ahead)  11.1 us
    dot_general x1, matrix products, orthogonal_step(): jnp.einsum('efg,egd->efd', combined, weight_grad, preferred_element_type=...  10.3 us
    ppermute x4, waiting for transfers between devices, spread_small(): other = lax.ppermute(gathered, AXIS, [(i, i ^ bit) for i in range(devices)])  8.68 us
    ppermute x3, waiting for transfers between devices, local(): left = lax.ppermute(left, AXIS, behind)  7.48 us
    dot_general x1, matrix products, orthogonal_step(): jnp.einsum('efd,egd->efg', weight_grad, weight_grad, preferred_element_ty...  7.26 us
  transfers between devices with their start and end apart: 22, of which 7 were waited for; matrix products, arithmetic and copies ran while one was open for 33% of the time, Pallas kernels for 17%

profile of v1, /device:TPU:15, one launch (start us, length us, event | category | flops | bytes accessed | tf_op | source)
XLA Modules:
  0.0 176.5 jit_solution(15154593506896932223)
XLA Ops:
  1.4 1.3 collective-permute-start.4
  7.4 1.1 slice_bitcast_fusion.26
  9.3 1.6 fusion.11
  11.2 3.2 %copy.45 = bf16[2,16,2,24,768]{4,3,2,1,0:T(8,128)(2,1)} copy(bf16[2,16,2,24,768]{4,3,1,0,2:T(8,128)(2,1)} %bitcast.104) | data formatting | bytes 4718592 | tf_op jit(solution)/shard_map/transpose | solution.py:284
  15.5 2.5 %collective-permute-done.11 = f32[2,2,2,8,64]{4,3,2,1,0:T(8,128)S(1)} collective-permute-done((f32[2,2,2,8,64]{4,3,2,1,0:T(8,128)S(1)}, f32[2,2,2,8,64]{4,3,2,1,0:T(8,128)S(1)}, u32[]{:S(2)}, u32[]{:S(2)}) %collective-permute-start.11) | collective-permute-done | bytes 16416 | tf_op jit(solution)/shard_map/ppermute | solution.py:70
  18.3 2.9 %collective-permute-done.12 = f32[4,2,2,8,64]{4,3,2,1,0:T(8,128)S(1)} collective-permute-done((f32[4,2,2,8,64]{4,3,2,1,0:T(8,128)S(1)}, f32[4,2,2,8,64]{4,3,2,1,0:T(8,128)S(1)}, u32[]{:S(2)}, u32[]{:S(2)}) %collective-permute-start.12) | collective-permute-done | bytes 32800 | tf_op jit(solution)/shard_map/ppermute | solution.py:70
  21.3 2.4 %collective-permute-start.13 = (f32[8,2,2,8,64]{4,3,2,1,0:T(8,128)S(1)}, f32[8,2,2,8,64]{4,3,2,1,0:T(8,128)S(1)}, u32[]{:S(2)}, u32[]{:S(2)}) collective-permute-start(f32[8,2,2,8,64]{4,3,2,1,0:T(8,128)S(1)} %pad_maximum_fusion), channel_id=1, source_target_pairs={{0,8},{1,9},{2,10},{3,11},{4,12},{5,13},{6,14},{7,15},{8,0},{9,1},... | collective-permute-start | bytes 196616 | tf_op jit(solution)/shard_map/ppermute | solution.py:70
  23.7 3.2 %collective-permute-done.13 = f32[8,2,2,8,64]{4,3,2,1,0:T(8,128)S(1)} collective-permute-done((f32[8,2,2,8,64]{4,3,2,1,0:T(8,128)S(1)}, f32[8,2,2,8,64]{4,3,2,1,0:T(8,128)S(1)}, u32[]{:S(2)}, u32[]{:S(2)}) %collective-permute-start.13) | collective-permute-done | bytes 65568 | tf_op jit(solution)/shard_map/ppermute | solution.py:70
  28.0 0.9 and.35
  29.8 1.1 select_reduce_fusion
  31.2 3.3 %collective-permute-start.19 = (bf16[2,64,2048]{2,1,0:T(8,128)(2,1)S(1)}, bf16[2,64,2048]{2,1,0:T(8,128)(2,1)S(1)}, u32[]{:S(2)}, u32[]{:S(2)}) collective-permute-start(bf16[2,64,2048]{2,1,0:T(8,128)(2,1)S(1)} %collective-permute-done.4), channel_id=1, source_target_pairs={{0,1},{1,0},{2,3},{3,2},{4,5},{5,4},{6,7},{7,6},{8,9},{9,8},{10,11... | collective-permute-start | bytes 1572872 | tf_op jit(solution)/shard_map/ppermute | solution.py:251
  34.5 0.9 collective-permute-start.5
  36.4 6.2 %expert_rows_2.2 = (bf16[2,16,48,2048]{3,2,1,0:T(8,128)(2,1)S(1)}, bf16[16,2,48,768]{3,2,1,0:T(8,128)(2,1)}) custom-call(s32[2]{0:T(128)S(1)} %get-tuple-element.58.ids_ref, s32[1]{0:T(128)} %bitcast.1.me_ref, bf16[64,2048]{1,0:T(8,128)(2,1)S(1)} %get-tuple-element.27.refs_0_, bf16[64,2048]{1,0:T(8,128)(2,1)S(1)} %get-tuple-element.26.refs_1_, ...), custom_call_target="tpu_custom_call" | custom-call | flops 704643072 | bytes 8421376 | tf_op jit(solution)/shard_map/expert_rows_2/pallas_call | solution.py:157
  42.6 7.7 %collective-permute-done.1 = bf16[2,64,2048]{2,1,0:T(8,128)(2,1)S(1)} collective-permute-done((bf16[2,64,2048]{2,1,0:T(8,128)(2,1)S(1)}, bf16[2,64,2048]{2,1,0:T(8,128)(2,1)S(1)}, u32[]{:S(2)}, u32[]{:S(2)}) %collective-permute-start.1) | collective-permute-done | bytes 524320 | tf_op jit(solution)/shard_map/ppermute | solution.py:259
  51.2 8.0 %expert_rows_4.3 = (bf16[2,16,48,2048]{3,2,1,0:T(8,128)(2,1)S(1)}, bf16[16,2,48,768]{3,2,1,0:T(8,128)(2,1)}) custom-call(s32[4]{0:T(128)S(1)} %get-tuple-element.60.ids_ref, s32[1]{0:T(128)} %bitcast.1.me_ref, bf16[64,2048]{1,0:T(8,128)(2,1)S(1)} %get-tuple-element.35.refs_0_, ...), custom_call_target="tpu_custom_call", output_to_operand_aliasing={{0}: (13, {}), {1}: (14, {})} | custom-call | flops 1409286144 | bytes 10551296 | tf_op jit(solution)/shard_map/expert_rows_4/pallas_call | solution.py:157
  59.4 1.8 %collective-permute-start.6 = (bf16[2,64,2048]{2,1,0:T(8,128)(2,1)S(1)}, bf16[2,64,2048]{2,1,0:T(8,128)(2,1)S(1)}, u32[]{:S(2)}, u32[]{:S(2)}) collective-permute-start(bf16[2,64,2048]{2,1,0:T(8,128)(2,1)S(1)} %collective-permute-done.5), channel_id=1, source_target_pairs={{0,2},{1,3},{4,0},{5,1},{8,4},{9,5},{12,8},{13,9},{14,12},{15,13},... | collective-permute-start | bytes 1572872 | tf_op jit(solution)/shard_map/ppermute | solution.py:260
  61.2 3.4 %collective-permute-done.2 = bf16[2,64,2048]{2,1,0:T(8,128)(2,1)S(1)} collective-permute-done((bf16[2,64,2048]{2,1,0:T(8,128)(2,1)S(1)}, bf16[2,64,2048]{2,1,0:T(8,128)(2,1)S(1)}, u32[]{:S(2)}, u32[]{:S(2)}) %collective-permute-start.2) | collective-permute-done | bytes 524320 | tf_op jit(solution)/shard_map/ppermute | solution.py:259
  64.9 7.5 %collective-permute-done.6 = bf16[2,64,2048]{2,1,0:T(8,128)(2,1)S(1)} collective-permute-done((bf16[2,64,2048]{2,1,0:T(8,128)(2,1)S(1)}, bf16[2,64,2048]{2,1,0:T(8,128)(2,1)S(1)}, u32[]{:S(2)}, u32[]{:S(2)}) %collective-permute-start.6) | collective-permute-done | bytes 524320 | tf_op jit(solution)/shard_map/ppermute | solution.py:260
  72.4 2.3 %collective-permute-start.7 = (bf16[64,2048]{1,0:T(8,128)(2,1)S(1)}, bf16[64,2048]{1,0:T(8,128)(2,1)S(1)}, u32[]{:S(2)}, u32[]{:S(2)}) collective-permute-start(bf16[64,2048]{1,0:T(8,128)(2,1)S(1)} %get-tuple-element.47.refs_5_), channel_id=1, source_target_pairs={{0,2},{1,3},{4,0},{5,1},{8,4},{9,5},{12,8},{13,9},{14,12},{15,13},... | collective-permute-start | bytes 786440 | tf_op jit(solution)/shard_map/ppermute | solution.py:262
  74.7 1.3 collective-permute-start.15
  76.2 8.0 %expert_rows_4.4 = (bf16[2,16,48,2048]{3,2,1,0:T(8,128)(2,1)S(1)}, bf16[16,2,48,768]{3,2,1,0:T(8,128)(2,1)}) custom-call(s32[4]{0:T(128)S(1)} %get-tuple-element.61.ids_ref, s32[1]{0:T(128)} %bitcast.1.me_ref, bf16[64,2048]{1,0:T(8,128)(2,1)S(1)} %get-tuple-element.43.refs_0_, ...), custom_call_target="tpu_custom_call", output_to_operand_aliasing={{0}: (13, {}), {1}: (14, {})} | custom-call | flops 1409286144 | bytes 10551296 | tf_op jit(solution)/shard_map/expert_rows_4/pallas_call | solution.py:157
  85.0 8.0 %expert_rows_4.5 = (bf16[2,16,48,2048]{3,2,1,0:T(8,128)(2,1)S(1)}, bf16[16,2,48,768]{3,2,1,0:T(8,128)(2,1)}) custom-call(s32[4]{0:T(128)S(1)} %get-tuple-element.62.ids_ref, s32[1]{0:T(128)} %bitcast.1.me_ref, bf16[64,2048]{1,0:T(8,128)(2,1)S(1)} %get-tuple-element.51.refs_0_, ...), custom_call_target="tpu_custom_call", output_to_operand_aliasing={{0}: (13, {}), {1}: (14, {})} | custom-call | flops 1409286144 | bytes 10551296 | tf_op jit(solution)/shard_map/expert_rows_4/pallas_call | solution.py:157
  93.1 6.2 %expert_rows_2.3 = (bf16[2,16,48,2048]{3,2,1,0:T(8,128)(2,1)S(1)}, bf16[16,2,48,768]{3,2,1,0:T(8,128)(2,1)}) custom-call(s32[2]{0:T(128)S(1)} %get-tuple-element.59.ids_ref, s32[1]{0:T(128)} %bitcast.1.me_ref, bf16[64,2048]{1,0:T(8,128)(2,1)S(1)} %collective-permute-done.3.refs_0_, ...), custom_call_target="tpu_custom_call", output_to_operand_aliasing={{0}: (9, {}), {1}: (10, {})} | custom-call | flops 704643072 | bytes 8421376 | tf_op jit(solution)/shard_map/expert_rows_2/pallas_call | solution.py:157
  99.3 5.6 %convolution_convert_fusion.1 = bf16[2,2048,768]{2,1,0:T(8,128)(2,1)S(1)} fusion(bf16[2,768,2048]{2,1,0:T(8,128)(2,1)S(1)} %bitcast.103, bf16[2,768,768]{2,1,0:T(8,128)(2,1)S(1)} %bitcast.105), kind=kOutput, calls=%fused_computation.7 | convolution fusion | flops 4834983936 | bytes 14942208 | tf_op jit(solution)/shard_map/jsf,jsd->jfd/dot_general | solution.py:285
  104.9 7.3 %multiply_reduce_fusion = (f32[2]{0:T(128)S(1)}, f32[2,768,768]{2,1,0:T(8,128)}) fusion(bf16[2,2048,768]{2,1,0:T(8,128)(2,1)S(1)} %convolution_convert_fusion.1), kind=kOutput, calls=%fused_computation.5 | convolution fusion | flops 4834197504 | bytes 11010056 | tf_op jit(solution)/shard_map/efd,egd->efg/dot_general | solution.py:216
  112.2 5.6 %all-to-all-start = ((bf16[16,2,48,768]{3,2,1,0:T(8,128)(2,1)}), bf16[16,2,48,768]{3,2,1,0:T(8,128)(2,1)}, u32[]{:S(2)}, u32[]{:S(2)}) async-start(bf16[16,2,48,768]{3,2,1,0:T(8,128)(2,1)} %get-tuple-element.20), calls=%async_computation | async-start | bytes 4718592 | tf_op jit(solution)/shard_map/all_to_all | solution.py:281
  117.7 9.2 %add_convert_fusion.1 = bf16[2,768,768]{2,1,0:T(8,128)(2,1)} fusion(f32[768,768]{1,0:T(8,128)S(1)} %copy-done, f32[2,768,768]{2,1,0:T(8,128)} %get-tuple-element.64, f32[2]{0:T(128)S(1)} %get-tuple-element.57), kind=kOutput, calls=%fused_computation.4 | convolution fusion | flops 1821376512 | bytes 9437192 | tf_op jit(solution)/shard_map/efg,egh->efh/dot_general | solution.py:223
  126.9 9.8 %fusion.6 = f32[2,768,768]{2,1,0:T(8,128)} fusion(bf16[2,768,768]{2,1,0:T(8,128)(2,1)} %add_convert_fusion.1, f32[2,768,768]{2,1,0:T(8,128)} %get-tuple-element.64, f32[2]{0:T(128)S(1)} %get-tuple-element.57), kind=kOutput, calls=%fused_computation.13 | convolution fusion | flops 3627417600 | bytes 11796488 | tf_op jit(solution)/shard_map/efg,egh->efh/dot_general | solution.py:223
  136.7 12.6 %fusion.2 = f32[2,768,768]{2,1,0:T(8,128)} fusion(bf16[2,768,768]{2,1,0:T(8,128)(2,1)} %add_convert_fusion.1, f32[2,768,768]{2,1,0:T(8,128)} %fusion.6, f32[768,768]{1,0:T(8,128)S(1)} %copy-done), kind=kOutput, calls=%fused_computation.9 | convolution fusion | flops 3630956544 | bytes 14155776 | tf_op jit(solution)/shard_map/efg,egh->efh/dot_general | solution.py:223
  149.3 10.3 %convolution_convert_fusion = bf16[2,768,2048]{2,1,0:T(8,128)(2,1)} fusion(bf16[2,2048,768]{2,1,0:T(8,128)(2,1)} %copy-done.3, f32[2,768,768]{2,1,0:T(8,128)} %fusion.2, f32[2]{0:T(128)S(1)} %get-tuple-element.56), kind=kOutput, calls=%fused_computation.6 | convolution fusion | flops 4837343232 | bytes 17301512 | tf_op jit(solution)/shard_map/efg,egd->efd/dot_general | solution.py:234
  159.7 11.2 %all-to-all-done = bf16[16,2,48,768]{3,2,1,0:T(8,128)(2,1)} async-done(((bf16[16,2,48,768]{3,2,1,0:T(8,128)(2,1)}), bf16[16,2,48,768]{3,2,1,0:T(8,128)(2,1)}, u32[]{:S(2)}, u32[]{:S(2)}) %all-to-all-start) | async-done | bytes 2359328 | tf_op jit(solution)/shard_map/all_to_all | solution.py:281
  170.9 5.7 %fusion.16 = bf16[1024,768]{1,0:T(8,128)(2,1)} fusion(bf16[1536,768]{1,0:T(8,128)(2,1)} %bitcast.43, s32[1024]{0:T(1024)S(1)} %copy-done.2), kind=kOutput, calls=%fused_computation.21 | convolution fusion | flops 2418278400 | bytes 3936256 | tf_op jit(solution)/shard_map/dot_general | solution.py:296
  (85 shorter events, 13.4 us)
Async XLA Ops:
  0.6 35.7 %collective-permute-start.20 = (bf16[2,64,2048]{2,1,0:T(8,128)(2,1)}, bf16[2,64,2048]{2,1,0:T(8,128)(2,1)S(1)}, u32[]{:S(2)}, u32[]{:S(2)}) collective-permute-start(bf16[2,64,2048]{2,1,0:T(8,128)(2,1)} %param.8), channel_id=1, source_target_pairs={{0,1},{1,0},{2,3},{3,2},{4,5},{5,4},{6,7},{7,6},{8,9},{9,8},{10,11... | collective-permute-start | bytes 1572872 | tf_op jit(solution)/shard_map/ppermute | solution.py:251
  1.4 29.8 %collective-permute-start.4 = (bf16[2,64,2048]{2,1,0:T(8,128)(2,1)}, bf16[2,64,2048]{2,1,0:T(8,128)(2,1)S(1)}, u32[]{:S(2)}, u32[]{:S(2)}) collective-permute-start(bf16[2,64,2048]{2,1,0:T(8,128)(2,1)} %param.8), channel_id=1, source_target_pairs={{0,2},{1,3},{4,0},{5,1},{8,4},{9,5},{12,8},{13,9},{14,12},{15,13},... | collective-permute-start | bytes 1572872 | tf_op jit(solution)/shard_map/ppermute | solution.py:260
  2.7 32.7 %collective-permute-start = (bf16[2,64,2048]{2,1,0:T(8,128)(2,1)}, bf16[2,64,2048]{2,1,0:T(8,128)(2,1)S(1)}, u32[]{:S(2)}, u32[]{:S(2)}) collective-permute-start(bf16[2,64,2048]{2,1,0:T(8,128)(2,1)} %param.8), channel_id=1, source_target_pairs={{0,4},{1,5},{4,8},{5,9},{8,12},{9,13},{12,14},{13,15},{14,10},{15,... | collective-permute-start | bytes 1572872 | tf_op jit(solution)/shard_map/ppermute | solution.py:259
  6.1 9.1 %collective-permute-start.10 = (f32[1,2,2,8,64]{4,3,2,1,0:T(8,128)S(1)}, f32[1,2,2,8,64]{4,3,2,1,0:T(8,128)S(1)}, u32[]{:S(2)}, u32[]{:S(2)}) collective-permute-start(f32[1,2,2,8,64]{4,3,2,1,0:T(8,128)S(1)} %maximum_bitcast_fusion), channel_id=1, source_target_pairs={{0,1},{1,0},{2,3},{3,2},{4,5},{5,4},{6,7},{7,6},{8,9},{9,8},{10,11... | collective-permute-start | bytes 24584 | tf_op jit(solution)/shard_map/ppermute | solution.py:70
  15.2 2.8 %collective-permute-start.11 = (f32[2,2,2,8,64]{4,3,2,1,0:T(8,128)S(1)}, f32[2,2,2,8,64]{4,3,2,1,0:T(8,128)S(1)}, u32[]{:S(2)}, u32[]{:S(2)}) collective-permute-start(f32[2,2,2,8,64]{4,3,2,1,0:T(8,128)S(1)} %pad_maximum_fusion.2), channel_id=1, source_target_pairs={{0,2},{1,3},{2,0},{3,1},{4,6},{5,7},{6,4},{7,5},{8,10},{9,11},{10,... | collective-permute-start | bytes 49160 | tf_op jit(solution)/shard_map/ppermute | solution.py:70
  18.1 3.2 %collective-permute-start.12 = (f32[4,2,2,8,64]{4,3,2,1,0:T(8,128)S(1)}, f32[4,2,2,8,64]{4,3,2,1,0:T(8,128)S(1)}, u32[]{:S(2)}, u32[]{:S(2)}) collective-permute-start(f32[4,2,2,8,64]{4,3,2,1,0:T(8,128)S(1)} %pad_maximum_fusion.1), channel_id=1, source_target_pairs={{0,4},{1,5},{2,6},{3,7},{4,0},{5,1},{6,2},{7,3},{8,12},{9,13},{10,... | collective-permute-start | bytes 98312 | tf_op jit(solution)/shard_map/ppermute | solution.py:70
  21.3 5.6 %collective-permute-start.13 = (f32[8,2,2,8,64]{4,3,2,1,0:T(8,128)S(1)}, f32[8,2,2,8,64]{4,3,2,1,0:T(8,128)S(1)}, u32[]{:S(2)}, u32[]{:S(2)}) collective-permute-start(f32[8,2,2,8,64]{4,3,2,1,0:T(8,128)S(1)} %pad_maximum_fusion), channel_id=1, source_target_pairs={{0,8},{1,9},{2,10},{3,11},{4,12},{5,13},{6,14},{7,15},{8,0},{9,1},... | collective-permute-start | bytes 196616 | tf_op jit(solution)/shard_map/ppermute | solution.py:70
  31.2 19.9 %collective-permute-start.19 = (bf16[2,64,2048]{2,1,0:T(8,128)(2,1)S(1)}, bf16[2,64,2048]{2,1,0:T(8,128)(2,1)S(1)}, u32[]{:S(2)}, u32[]{:S(2)}) collective-permute-start(bf16[2,64,2048]{2,1,0:T(8,128)(2,1)S(1)} %collective-permute-done.4), channel_id=1, source_target_pairs={{0,1},{1,0},{2,3},{3,2},{4,5},{5,4},{6,7},{7,6},{8,9},{9,8},{10,11... | collective-permute-start | bytes 1572872 | tf_op jit(solution)/shard_map/ppermute | solution.py:251
  34.5 24.8 %collective-permute-start.5 = (bf16[2,64,2048]{2,1,0:T(8,128)(2,1)S(1)}, bf16[2,64,2048]{2,1,0:T(8,128)(2,1)S(1)}, u32[]{:S(2)}, u32[]{:S(2)}) collective-permute-start(bf16[2,64,2048]{2,1,0:T(8,128)(2,1)S(1)} %collective-permute-done.4), channel_id=1, source_target_pairs={{0,2},{1,3},{4,0},{5,1},{8,4},{9,5},{12,8},{13,9},{14,12},{15,13},... | collective-permute-start | bytes 1572872 | tf_op jit(solution)/shard_map/ppermute | solution.py:260
  35.4 15.8 %collective-permute-start.18 = (bf16[2,64,2048]{2,1,0:T(8,128)(2,1)S(1)}, bf16[2,64,2048]{2,1,0:T(8,128)(2,1)S(1)}, u32[]{:S(2)}, u32[]{:S(2)}) collective-permute-start(bf16[2,64,2048]{2,1,0:T(8,128)(2,1)S(1)} %collective-permute-done), channel_id=1, source_target_pairs={{0,1},{1,0},{2,3},{3,2},{4,5},{5,4},{6,7},{7,6},{8,9},{9,8},{10,11... | collective-permute-start | bytes 1572872 | tf_op jit(solution)/shard_map/ppermute | solution.py:251
  35.7 14.6 %collective-permute-start.1 = (bf16[2,64,2048]{2,1,0:T(8,128)(2,1)S(1)}, bf16[2,64,2048]{2,1,0:T(8,128)(2,1)S(1)}, u32[]{:S(2)}, u32[]{:S(2)}) collective-permute-start(bf16[2,64,2048]{2,1,0:T(8,128)(2,1)S(1)} %collective-permute-done), channel_id=1, source_target_pairs={{0,4},{1,5},{4,8},{5,9},{8,12},{9,13},{12,14},{13,15},{14,10},{15,... | collective-permute-start | bytes 1572872 | tf_op jit(solution)/shard_map/ppermute | solution.py:259
  50.3 25.8 %collective-permute-start.16 = (bf16[2,64,2048]{2,1,0:T(8,128)(2,1)S(1)}, bf16[2,64,2048]{2,1,0:T(8,128)(2,1)S(1)}, u32[]{:S(2)}, u32[]{:S(2)}) collective-permute-start(bf16[2,64,2048]{2,1,0:T(8,128)(2,1)S(1)} %collective-permute-done.1), channel_id=1, source_target_pairs={{0,1},{1,0},{2,3},{3,2},{4,5},{5,4},{6,7},{7,6},{8,9},{9,8},{10,11... | collective-permute-start | bytes 1572872 | tf_op jit(solution)/shard_map/ppermute | solution.py:251
  51.1 13.5 %collective-permute-start.2 = (bf16[2,64,2048]{2,1,0:T(8,128)(2,1)S(1)}, bf16[2,64,2048]{2,1,0:T(8,128)(2,1)S(1)}, u32[]{:S(2)}, u32[]{:S(2)}) collective-permute-start(bf16[2,64,2048]{2,1,0:T(8,128)(2,1)S(1)} %collective-permute-done.1), channel_id=1, source_target_pairs={{0,4},{1,5},{4,8},{5,9},{8,12},{9,13},{12,14},{13,15},{14,10},{15,... | collective-permute-start | bytes 1572872 | tf_op jit(solution)/shard_map/ppermute | solution.py:259
  59.2 16.8 %collective-permute-start.17 = (bf16[2,64,2048]{2,1,0:T(8,128)(2,1)S(1)}, bf16[2,64,2048]{2,1,0:T(8,128)(2,1)S(1)}, u32[]{:S(2)}, u32[]{:S(2)}) collective-permute-start(bf16[2,64,2048]{2,1,0:T(8,128)(2,1)S(1)} %collective-permute-done.5), channel_id=1, source_target_pairs={{0,1},{1,0},{2,3},{3,2},{4,5},{5,4},{6,7},{7,6},{8,9},{9,8},{10,11... | collective-permute-start | bytes 1572872 | tf_op jit(solution)/shard_map/ppermute | solution.py:251
  59.4 13.0 %collective-permute-start.6 = (bf16[2,64,2048]{2,1,0:T(8,128)(2,1)S(1)}, bf16[2,64,2048]{2,1,0:T(8,128)(2,1)S(1)}, u32[]{:S(2)}, u32[]{:S(2)}) collective-permute-start(bf16[2,64,2048]{2,1,0:T(8,128)(2,1)S(1)} %collective-permute-done.5), channel_id=1, source_target_pairs={{0,2},{1,3},{4,0},{5,1},{8,4},{9,5},{12,8},{13,9},{14,12},{15,13},... | collective-permute-start | bytes 1572872 | tf_op jit(solution)/shard_map/ppermute | solution.py:260
  64.6 19.6 %collective-permute-start.3 = (bf16[64,2048]{1,0:T(8,128)(2,1)S(1)}, bf16[64,2048]{1,0:T(8,128)(2,1)S(1)}, u32[]{:S(2)}, u32[]{:S(2)}) collective-permute-start(bf16[64,2048]{1,0:T(8,128)(2,1)S(1)} %get-tuple-element.51.refs_0_), channel_id=1, source_target_pairs={{0,4},{1,5},{4,8},{5,9},{8,12},{9,13},{12,14},{13,15},{14,10},{15,... | collective-permute-start | bytes 786440 | tf_op jit(solution)/shard_map/ppermute | solution.py:262
  72.4 12.3 %collective-permute-start.7 = (bf16[64,2048]{1,0:T(8,128)(2,1)S(1)}, bf16[64,2048]{1,0:T(8,128)(2,1)S(1)}, u32[]{:S(2)}, u32[]{:S(2)}) collective-permute-start(bf16[64,2048]{1,0:T(8,128)(2,1)S(1)} %get-tuple-element.47.refs_5_), channel_id=1, source_target_pairs={{0,2},{1,3},{4,0},{5,1},{8,4},{9,5},{12,8},{13,9},{14,12},{15,13},... | collective-permute-start | bytes 786440 | tf_op jit(solution)/shard_map/ppermute | solution.py:262
  74.7 10.2 %collective-permute-start.15 = (bf16[2,64,2048]{2,1,0:T(8,128)(2,1)S(1)}, bf16[2,64,2048]{2,1,0:T(8,128)(2,1)S(1)}, u32[]{:S(2)}, u32[]{:S(2)}) collective-permute-start(bf16[2,64,2048]{2,1,0:T(8,128)(2,1)S(1)} %collective-permute-done.6), channel_id=1, source_target_pairs={{0,1},{1,0},{2,3},{3,2},{4,5},{5,4},{6,7},{7,6},{8,9},{9,8},{10,11... | collective-permute-start | bytes 1572872 | tf_op jit(solution)/shard_map/ppermute | solution.py:251
  76.0 8.9 %collective-permute-start.14 = (bf16[2,64,2048]{2,1,0:T(8,128)(2,1)S(1)}, bf16[2,64,2048]{2,1,0:T(8,128)(2,1)S(1)}, u32[]{:S(2)}, u32[]{:S(2)}) collective-permute-start(bf16[2,64,2048]{2,1,0:T(8,128)(2,1)S(1)} %collective-permute-done.2), channel_id=1, source_target_pairs={{0,1},{1,0},{2,3},{3,2},{4,5},{5,4},{6,7},{7,6},{8,9},{9,8},{10,11... | collective-permute-start | bytes 1572872 | tf_op jit(solution)/shard_map/ppermute | solution.py:251
  84.2 8.8 %collective-permute-start.8 = (bf16[64,2048]{1,0:T(8,128)(2,1)S(1)}, bf16[64,2048]{1,0:T(8,128)(2,1)S(1)}, u32[]{:S(2)}, u32[]{:S(2)}) collective-permute-start(bf16[64,2048]{1,0:T(8,128)(2,1)S(1)} %collective-permute-done.3.refs_0_), channel_id=1, source_target_pairs={{0,1},{1,0},{2,3},{3,2},{4,5},{5,4},{6,7},{7,6},{8,9},{9,8},{10,11... | collective-permute-start | bytes 786440 | tf_op jit(solution)/shard_map/ppermute | solution.py:251
  84.8 8.3 %collective-permute-start.9 = (bf16[64,2048]{1,0:T(8,128)(2,1)S(1)}, bf16[64,2048]{1,0:T(8,128)(2,1)S(1)}, u32[]{:S(2)}, u32[]{:S(2)}) collective-permute-start(bf16[64,2048]{1,0:T(8,128)(2,1)S(1)} %collective-permute-done.7.refs_1_), channel_id=1, source_target_pairs={{0,1},{1,0},{2,3},{3,2},{4,5},{5,4},{6,7},{7,6},{8,9},{9,8},{10,11... | collective-permute-start | bytes 786440 | tf_op jit(solution)/shard_map/ppermute | solution.py:251
  93.0 6.2 %copy-start.1 = (bf16[2,16,2,24,768]{4,3,2,1,0:T(8,128)(2,1)S(1)}, bf16[2,16,2,24,768]{4,3,2,1,0:T(8,128)(2,1)}, u32[]{:S(2)}) copy-start(bf16[2,16,2,24,768]{4,3,2,1,0:T(8,128)(2,1)} %copy.45) | copy-start | bytes 7077892
  104.9 7.3 %copy-start.3 = (bf16[2,2048,768]{2,1,0:T(8,128)(2,1)}, bf16[2,2048,768]{2,1,0:T(8,128)(2,1)S(1)}, u32[]{:S(2)}) copy-start(bf16[2,2048,768]{2,1,0:T(8,128)(2,1)S(1)} %convolution_convert_fusion.1) | copy-start | bytes 18874372
  112.1 5.6 %copy-start = (f32[768,768]{1,0:T(8,128)S(1)}, f32[768,768]{1,0:T(8,128)}, u32[]{:S(2)}) copy-start(f32[768,768]{1,0:T(8,128)} %fusion.11) | copy-start | bytes 7077892
  112.2 58.7 %all-to-all-start = ((bf16[16,2,48,768]{3,2,1,0:T(8,128)(2,1)}), bf16[16,2,48,768]{3,2,1,0:T(8,128)(2,1)}, u32[]{:S(2)}, u32[]{:S(2)}) async-start(bf16[16,2,48,768]{3,2,1,0:T(8,128)(2,1)} %get-tuple-element.20), calls=%async_computation | async-start | bytes 4718592 | tf_op jit(solution)/shard_map/all_to_all | solution.py:281
  149.3 21.5 %copy-start.2 = (s32[1024]{0:T(1024)S(1)}, s32[1024]{0:T(1024)}, u32[]{:S(2)}) copy-start(s32[1024]{0:T(1024)} %eq.79) | copy-start | bytes 12292

commit v2 on v1

v2 whole, which is shorter than its diff:
```python
import functools
import math

import jax
import jax.numpy as jnp
import numpy as np
from jax import lax
from jax.experimental import pallas as pl
from jax.experimental.pallas import tpu as pltpu
from jax.sharding import PartitionSpec as P


COEF_A = 3.4445
COEF_B = -4.775
COEF_C = 2.0315
AXIS = "expert"
META = 8
NN = (((1,), (0,)), ((), ()))
NT = (((1,), (1,)), ((), ()))
TN = (((0,), (0,)), ((), ()))
ANY = pl.BlockSpec(memory_space=pl.ANY)
HBM = pl.BlockSpec(memory_space=pltpu.HBM)
SMEM = pl.BlockSpec(memory_space=pltpu.SMEM)


def ring_layout(mesh):
    row = np.asarray(mesh.devices)[0].reshape(-1)
    chips = len(row) // 2
    coords = [getattr(d, "coords", None) for d in row[::2]]
    if any(c is None for c in coords):
        return list(range(chips))
    ys = sorted({c[1] for c in coords})
    if len(ys) != 2:
        return list(range(chips))
    first = [i for i in range(chips) if coords[i][1] == ys[0]]
    second = [i for i in range(chips) if coords[i][1] == ys[1]]
    first.sort(key=lambda i: coords[i][2])
    second.sort(key=lambda i: -coords[i][2])
    return first + second


def shift_pairs(order, step):
    chips = len(order)
    return [
        (order[p] * 2 + core, order[(p + step) % chips] * 2 + core)
        for p in range(chips)
        for core in range(2)
    ]


def swap_pairs(devices):
    return [(i, i ^ 1) for i in range(devices)]


def source_table(order):
    chips = len(order)
    place = {chip: p for p, chip in enumerate(order)}
    table = np.zeros((chips * 2, chips * 2), np.int32)
    for i in range(chips * 2):
        p, core = place[i // 2], i % 2
        steps = [0]
        for s in range(1, chips // 2):
            steps += [-s, s]
        steps.append(chips // 2)
        row = []
        for s in steps:
            chip = order[(p + s) % chips]
            row += [chip * 2 + core, chip * 2 + 1 - core]
        table[i] = row
    return table


def pack_kernel(routes_ref, gates_ref, tok_ref, out_ref):
    batches, top, tokens = routes_ref.shape
    total = batches * tokens
    width = tok_ref.shape[2]
    for m in range(batches):
        out_ref[m * tokens : (m + 1) * tokens, :] = tok_ref[m]
    routes = jnp.concatenate([routes_ref[m] for m in range(batches)], axis=1).astype(jnp.float32)
    gates = jnp.concatenate([gates_ref[m] for m in range(batches)], axis=1)
    parts = [routes]
    rest = gates
    for _ in range(3):
        part = rest.astype(jnp.bfloat16).astype(jnp.float32)
        parts.append(part)
        rest = rest - part
    parts.append(jnp.zeros((top, width - 4 * total), jnp.float32))
    meta = jnp.concatenate(parts, axis=1)
    out_ref[total : total + META, :] = meta.astype(jnp.bfloat16)


def pack(routes, gates, grad_out):
    batches, tokens, width = grad_out.shape
    return pl.pallas_call(
        pack_kernel,
        out_shape=jax.ShapeDtypeStruct((batches * tokens + META, width), jnp.bfloat16),
        name="pack",
    )(routes, gates, grad_out)


def expert_kernel(pieces, first, batches, ids_ref, me_ref, *refs):
    count = len(pieces)
    chunk_refs = []
    for n in pieces:
        chunk_refs.append(refs[:n])
        refs = refs[n:]
    if first:
        w_hbm, disp_out, grad_out = refs[:3]
        refs = refs[3:]
    else:
        w_hbm, _, _, disp_out, grad_out = refs[:5]
        refs = refs[5:]
    tok, w, rows, back, in_sem, w_sem, out_sem = refs
    width = tok.shape[2]
    total = tok.shape[1] - META
    tokens = total // batches
    part = rows.shape[1] // count
    capacity = part // batches
    hidden = w.shape[1]
    sources = [ids_ref[i] for i in range(count)]
    loads = []
    for i in range(count):
        now, at = [], 0
        for j, ref in enumerate(chunk_refs[i]):
            now.append(pltpu.make_async_copy(ref, tok.at[i, pl.ds(at, ref.shape[0])], in_sem.at[i, j]))
            at += ref.shape[0]
        for c in now:
            c.start()
        loads.append(now)
    w_loads = [pltpu.make_async_copy(w_hbm.at[e], w.at[e], w_sem.at[e]) for e in range(2)]
    for c in w_loads:
        c.start()
    token_at = lax.broadcasted_iota(jnp.int32, (total, total), 0)
    token_to = lax.broadcasted_iota(jnp.int32, (total, total), 1)
    before = ((token_at < token_to) & (token_at // tokens == token_to // tokens)).astype(jnp.bfloat16)
    row = lax.broadcasted_iota(jnp.int32, (part, total), 0)
    lane = lax.broadcasted_iota(jnp.int32, (part, total), 1)
    slot = (row % capacity).astype(jnp.float32)
    same = (row // capacity) == (lane // tokens)
    stores = []
    step = min(512, width)
    for i in range(count):
        for c in loads[i]:
            c.wait()
        meta = tok[i, total:, : 4 * total].astype(jnp.float32)
        routes = meta[:, :total]
        gates = meta[:, total : 2 * total] + meta[:, 2 * total : 3 * total] + meta[:, 3 * total :]
        picks, columns = [], []
        for e in range(2):
            hit = routes == (2 * me_ref[0] + e).astype(jnp.float32)
            named = jnp.sum(jnp.where(hit, 1.0, 0.0), axis=0, keepdims=True)
            gate = jnp.sum(jnp.where(hit, gates, 0.0), axis=0, keepdims=True)
            rank = jnp.dot(
                jnp.broadcast_to(named, (8, total)).astype(jnp.bfloat16),
                before,
                preferred_element_type=jnp.float32,
            )[:1]
            pick = (rank == slot) & (named > 0.5) & same
            picks.append(jnp.where(pick, 1.0, 0.0).astype(jnp.bfloat16))
            columns.append(jnp.sum(jnp.where(pick, gate, 0.0), axis=1, keepdims=True))
        for at in range(0, width, step):
            for e in range(2):
                picked = jnp.dot(picks[e], tok[i, :total, at : at + step], preferred_element_type=jnp.float32)
                rows[e, i * part : (i + 1) * part, at : at + step] = (picked * columns[e]).astype(jnp.bfloat16)
        for e in range(2):
            c = pltpu.make_async_copy(
                rows.at[e, pl.ds(i * part, part)], disp_out.at[e, sources[i]], out_sem.at[i, e]
            )
            c.start()
            stores.append(c)
    for e in range(2):
        w_loads[e].wait()
        for at in range(0, hidden, 256):
            product = lax.dot_general(
                rows[e], w[e, at : at + 256, :], NT, preferred_element_type=jnp.float32
            ).astype(jnp.bfloat16)
            for i in range(count):
                back[i, e, :, at : at + 256] = product[i * part : (i + 1) * part]
    for i in range(count):
        c = pltpu.make_async_copy(back.at[i], grad_out.at[sources[i]], out_sem.at[i, 2])
        c.start()
        stores.append(c)
    for c in stores:
        c.wait()


def expert_rows(ids, me, chunks, weight, carried, devices, batches, capacity):
    operands = [x for pieces in chunks for x in pieces]
    width = weight.shape[2]
    hidden = weight.shape[1]
    part = batches * capacity
    count = len(chunks)
    total = sum(x.shape[0] for x in chunks[0])
    first = carried is None
    args = [ids, me, *operands, weight]
    aliases = {}
    if not first:
        aliases = {len(args): 0, len(args) + 1: 1}
        args += list(carried)
    flops = 4 * count * part * (total * width + width * hidden)
    moved = weight.size * 2 + count * (total * width + 2 * part * (width + hidden)) * 2
    return pl.pallas_call(
        functools.partial(expert_kernel, [len(x) for x in chunks], first, batches),
        out_shape=(
            jax.ShapeDtypeStruct((2, devices, part, width), jnp.bfloat16),
            jax.ShapeDtypeStruct((devices, 2, part, hidden), jnp.bfloat16),
        ),
        in_specs=[SMEM, SMEM] + [ANY] * len(operands) + [HBM] * (len(args) - 2 - len(operands)),
        out_specs=(HBM, HBM),
        scratch_shapes=[
            pltpu.VMEM((count, total, width), jnp.bfloat16),
            pltpu.VMEM((2, hidden, width), jnp.bfloat16),
            pltpu.VMEM((2, count * part, width), jnp.bfloat16),
            pltpu.VMEM((count, 2, part, hidden), jnp.bfloat16),
            pltpu.SemaphoreType.DMA((count, 2)),
            pltpu.SemaphoreType.DMA((2,)),
            pltpu.SemaphoreType.DMA((count, 3)),
        ],
        input_output_aliases=aliases,
        cost_estimate=pl.CostEstimate(flops=flops, bytes_accessed=moved, transcendentals=0),
        compiler_params=pltpu.CompilerParams(vmem_limit_bytes=32 << 20),
    )(*args)


def update_kernel(tile, disp_hbm, hid_hbm, out_hbm, disp, hid, wg, gram, half, poly, left, nxt, out, in_sem, out_sem):
    experts, total, width = disp_hbm.shape
    batches, _, _, _, hidden = hid_hbm.shape
    blocks = hidden // tile
    loads = []
    for e in range(experts):
        now = [pltpu.make_async_copy(disp_hbm.at[e], disp.at[e], in_sem.at[e, 0])]
        for m in range(batches):
            now.append(pltpu.make_async_copy(hid_hbm.at[m, e], hid.at[e, :, m], in_sem.at[e, 1 + m]))
        for c in now:
            c.start()
        loads.append(now)

    def rows(i):
        return pl.ds(pl.multiple_of(i * tile, tile), tile)

    def dot(a, b, dims=NN):
        return lax.dot_general(a, b, dims, preferred_element_type=jnp.float32)

    def diagonal(i):
        r = lax.broadcasted_iota(jnp.int32, (tile, hidden), 0) + i * tile
        return r == lax.broadcasted_iota(jnp.int32, (tile, hidden), 1)

    stores = []
    for e in range(experts):
        for c in loads[e]:
            c.wait()

        @pl.loop(0, blocks)
        def _(i):
            cols = pl.ds(pl.multiple_of(i * tile, tile), tile)
            h = hid[e, :, :, :, cols].reshape(total, tile)
            wg[rows(i), :] = dot(h, disp[e], TN).astype(jnp.bfloat16)

        def gram_rows(i, total_sq):
            g = dot(wg[rows(i), :], wg[...], NT)
            gram[rows(i), :] = g
            return total_sq + jnp.sum(g * g)

        norm = jnp.sqrt(lax.fori_loop(0, blocks, gram_rows, jnp.float32(0.0))) + 1e-06
        half[...] = (gram[...] / norm).astype(jnp.bfloat16)
        scale = COEF_B / norm

        @pl.loop(0, blocks)
        def _(i):
            square = dot(half[rows(i), :], half[...])
            p = COEF_C * square + scale * gram[rows(i), :]
            poly[rows(i), :] = jnp.where(diagonal(i), p + COEF_A, p).astype(jnp.bfloat16)

        @pl.loop(0, blocks)
        def _(i):
            left[rows(i), :] = dot(poly[rows(i), :], half[...]).astype(jnp.bfloat16)

        @pl.loop(0, blocks)
        def _(i):
            g = dot(left[rows(i), :], poly[...])
            gram[rows(i), :] = g
            nxt[rows(i), :] = g.astype(jnp.bfloat16)

        scaling = math.sqrt(width) / jnp.sqrt(norm)

        @pl.loop(0, blocks)
        def _(i):
            square = dot(nxt[rows(i), :], nxt[...])
            p = COEF_C * square + COEF_B * gram[rows(i), :]
            left[rows(i), :] = jnp.where(diagonal(i), p + COEF_A, p).astype(jnp.bfloat16)

        @pl.loop(0, blocks)
        def _(i):
            half[rows(i), :] = (dot(left[rows(i), :], poly[...]) * scaling).astype(jnp.bfloat16)

        @pl.loop(0, blocks)
        def _(i):
            out[e, rows(i), :] = dot(half[rows(i), :], wg[...]).astype(jnp.bfloat16)

        c = pltpu.make_async_copy(out.at[e], out_hbm.at[e], out_sem.at[e])
        c.start()
        stores.append(c)
    for c in stores:
        c.wait()


def expert_update(dispatched, saved_hidden, tile=768):
    experts, total, width = dispatched.shape
    batches, _, sources, capacity, hidden = saved_hidden.shape
    flops = 2 * experts * hidden * (width * (total + 2 * hidden) + 5 * hidden * hidden)
    moved = experts * (total * (width + hidden) + hidden * width) * 2
    square = (hidden, hidden)
    return pl.pallas_call(
        functools.partial(update_kernel, tile),
        out_shape=jax.ShapeDtypeStruct((experts, hidden, width), jnp.bfloat16),
        in_specs=[HBM, ANY],
        out_specs=HBM,
        scratch_shapes=[
            pltpu.VMEM((experts, total, width), jnp.bfloat16),
            pltpu.VMEM((experts, sources, batches, capacity, hidden), jnp.bfloat16),
            pltpu.VMEM((hidden, width), jnp.bfloat16),
            pltpu.VMEM(square, jnp.float32),
            pltpu.VMEM(square, jnp.bfloat16),
            pltpu.VMEM(square, jnp.bfloat16),
            pltpu.VMEM(square, jnp.bfloat16),
            pltpu.VMEM(square, jnp.bfloat16),
            pltpu.VMEM((experts, hidden, width), jnp.bfloat16),
            pltpu.SemaphoreType.DMA((experts, 1 + batches)),
            pltpu.SemaphoreType.DMA((experts,)),
        ],
        cost_estimate=pl.CostEstimate(flops=flops, bytes_accessed=moved, transcendentals=0),
        compiler_params=pltpu.CompilerParams(vmem_limit_bytes=48 << 20),
        name="expert_update",
    )(dispatched, saved_hidden)


def own_places(routes, experts, capacity):
    matches = (routes[..., None] == jnp.arange(experts, dtype=jnp.int32)).astype(jnp.int32)
    per_token = jnp.sum(matches, axis=2)
    earlier = jnp.cumsum(per_token, axis=1) - per_token
    slot = jnp.sum(matches * earlier[:, :, None, :], axis=3)
    batches = routes.shape[0]
    batch = jnp.arange(batches, dtype=jnp.int32)[:, None, None]
    return (routes * batches + batch) * capacity + slot


def local(order, routes, gate_weights, grad_out, saved_hidden, down_weight):
    devices = lax.axis_size(AXIS)
    me = lax.axis_index(AXIS)
    chips = devices // 2
    local_experts, hidden, width = down_weight.shape
    batches, tokens, top = routes.shape
    capacity = saved_hidden.shape[2] // devices
    experts = devices * local_experts
    ahead, behind, swap = shift_pairs(order, 1), shift_pairs(order, -1), swap_pairs(devices)

    def swapped(x):
        return lax.ppermute(x, AXIS, swap)

    chunk = pack(jnp.swapaxes(routes, 1, 2), jnp.swapaxes(gate_weights, 1, 2), grad_out)
    ids = jnp.asarray(source_table(order))[me]
    me1 = me.reshape(1).astype(jnp.int32)
    half = chips // 2
    right = left = chunk
    arrived = [[chunk]]
    for step in range(1, half + 1):
        right = lax.ppermute(right if step < half else right[:tokens], AXIS, ahead)
        left = lax.ppermute(left if step < half else left[tokens:], AXIS, behind)
        arrived.append([right, left])
    carried = None
    done = 0
    waiting = []
    for step, group in enumerate(arrived):
        others = []
        for x in group:
            others.append(swapped(x))
        if step < half:
            waiting += [(c,) for pair in zip(group, others) for c in pair]
        else:
            waiting += [tuple(group), tuple(others)]
        if step == half - 1:
            continue
        carried = expert_rows(
            ids[done : done + len(waiting)], me1, waiting, down_weight, carried, devices, batches, capacity
        )
        done += len(waiting)
        waiting = []
    dispatched, slot_grad = carried

    returned = lax.all_to_all(slot_grad, AXIS, split_axis=0, concat_axis=0, tiled=True)

    update = expert_update(
        dispatched.reshape(local_experts, -1, width),
        saved_hidden.reshape(batches, local_experts, devices, capacity, hidden),
    )

    places = own_places(routes, experts, capacity).reshape(-1, 1)
    table = returned.reshape(-1, hidden)
    chosen = (places == jnp.arange(table.shape[0], dtype=jnp.int32)[None]).astype(jnp.bfloat16)
    hidden_grad = jnp.dot(chosen, table, preferred_element_type=jnp.float32).astype(jnp.bfloat16)
    return hidden_grad.reshape(batches, tokens, top, hidden), update


def solution(mesh):
    in_specs = (
        P(None, ("groups", AXIS), None),
        P(None, ("groups", AXIS), None),
        P(None, ("groups", AXIS), None),
        P("groups", AXIS, None, None),
        P(AXIS, None, None),
    )
    out_specs = (P(None, ("groups", AXIS), None, None), P(AXIS, "groups", None))
    order = ring_layout(mesh)

    def body(*args):
        return local(order, *args)

    return jax.shard_map(body, mesh=mesh, in_specs=in_specs, out_specs=out_specs, check_vma=False)
```

time: 177 us -> 163 us (0.921)
  matrix products: 60.5 us -> 5.66 us
  Pallas kernels: 36.5 us -> 70.2 us
  waiting for transfers between devices: 38.5 us -> 56.5 us
  other arithmetic: 7.61 us -> 0.21 us
  starting transfers between devices: 23.7 us -> 21.1 us
    dot_general x7 -> x0, matrix products: 54.9 us -> none  [the longest x3 31.6 us: product(): return jnp.einsum('efg,egh->efh', a, b, preferred_element_type=jnp.float32)]
    pallas_call x5 -> x6, Pallas kernels: 36.5 us -> 70.2 us  [the longest x4 34.8 us: expert_rows(): pl.pallas_call(functools.partial(expert_kernel, [len(x) for x in chunks],...]
    ppermute x12 -> x8, waiting for transfers between devices: 27.2 us -> 37.4 us  [the longest x4 35.2 us: local(): left = lax.ppermute(left if step < half else left[tokens:], AXIS, behind)]
    all_to_all x1, waiting for transfers between devices: 11.2 us -> 19.1 us  [local(): lax.all_to_all(slot_grad, AXIS, split_axis=0, concat_axis=0, tiled=True)]
    unnamed x11 -> x12, local copies, waits for them, and re-layouts: 0.03 us -> 6.5 us
    ppermute x12 -> x8, starting transfers between devices: 10.9 us -> 5.92 us  [the longest x4 5.19 us: local(): left = lax.ppermute(left if step < half else left[tokens:], AXIS, behind)]
    transpose x1 -> x0, local copies, waits for them, and re-layouts: 3.25 us -> none  [local(): jnp.transpose(hidden_rows, (1, 2, 0, 3, 4))]
    ppermute x9, starting transfers between devices: 7.19 us -> 9.77 us  [swapped(): return lax.ppermute(x, AXIS, swap)]
  transfers between devices with their start and end apart: 22 -> 18, of which waited for: 7 -> 6; matrix products, arithmetic and copies ran while one was open for 33% -> 1% of each run, Pallas kernels for 17% -> 35%
where the time goes in v2:
time: 163 us; the launch traced here: 162 us
  Pallas kernels  70.2 us (43%)
  waiting for transfers between devices  56.5 us (35%)
  starting transfers between devices  21.1 us (13%)
  local copies, waits for them, and re-layouts  7.71 us (5%)
  matrix products  5.66 us (3%)
    ppermute x4, waiting for transfers between devices, local(): left = lax.ppermute(left if step < half else left[tokens:], AXIS, behind)  35.2 us
    pallas_call x4, Pallas kernels, expert_rows(): pl.pallas_call(functools.partial(expert_kernel, [len(x) for x in chunks],...  34.8 us
    pallas_call x1, Pallas kernels, expert_update(): pl.pallas_call(functools.partial(update_kernel, tile), out_shape=jax.Shap...  33.4 us
    all_to_all x1, waiting for transfers between devices, local(): lax.all_to_all(slot_grad, AXIS, split_axis=0, concat_axis=0, tiled=True)  19.1 us
    ppermute x9, starting transfers between devices, swapped(): return lax.ppermute(x, AXIS, swap)  9.77 us
    unnamed x12, local copies, waits for them, and re-layouts  6.5 us
    dot_general x1, matrix products, local(): jnp.dot(chosen, table, preferred_element_type=jnp.float32)  5.66 us
    all_to_all x1, starting transfers between devices, local(): lax.all_to_all(slot_grad, AXIS, split_axis=0, concat_axis=0, tiled=True)  5.4 us
  transfers between devices with their start and end apart: 18, of which 6 were waited for; matrix products, arithmetic and copies ran while one was open for 1% of the time, Pallas kernels for 35%

profile of v2, /device:TPU:15, one launch (start us, length us, event | category | flops | bytes accessed | tf_op | source)
XLA Modules:
  0.0 162.2 jit_solution(4720156183009498158)
XLA Ops:
  0.6 2.0 %pack.1.refs_0_ = bf16[136,2048]{1,0:T(8,128)(2,1)} custom-call(s32[2,8,64]{2,1,0:T(8,128)} %bitcast.18, f32[2,8,64]{2,1,0:T(8,128)} %bitcast.19, bf16[2,64,2048]{2,1,0:T(8,128)(2,1)} %tok_ref.1), custom_call_target="tpu_custom_call" | custom-call | tf_op jit(solution)/shard_map/pack/pallas_call | solution.py:94
  2.6 1.3 collective-permute-start.4
  3.9 0.2 collective-permute-start
  4.1 12.3 %collective-permute-done.4.refs_2_ = bf16[136,2048]{1,0:T(8,128)(2,1)S(1)} collective-permute-done((bf16[136,2048]{1,0:T(8,128)(2,1)}, bf16[136,2048]{1,0:T(8,128)(2,1)S(1)}, u32[]{:S(2)}, u32[]{:S(2)}) %collective-permute-start.4) | collective-permute-done | bytes 557088 | tf_op jit(solution)/shard_map/ppermute | solution.py:368
  16.3 1.3 collective-permute-start.5
  17.6 0.2 collective-permute-start.1
  17.8 11.2 %collective-permute-done.5.refs_2_ = bf16[136,2048]{1,0:T(8,128)(2,1)S(1)} collective-permute-done((bf16[136,2048]{1,0:T(8,128)(2,1)S(1)}, bf16[136,2048]{1,0:T(8,128)(2,1)S(1)}, u32[]{:S(2)}, u32[]{:S(2)}) %collective-permute-start.5) | collective-permute-done | bytes 557088 | tf_op jit(solution)/shard_map/ppermute | solution.py:368
  29.0 1.3 collective-permute-start.6
  30.3 2.7 %collective-permute-start.16 = (bf16[136,2048]{1,0:T(8,128)(2,1)}, bf16[136,2048]{1,0:T(8,128)(2,1)}, u32[]{:S(2)}, u32[]{:S(2)}) collective-permute-start(bf16[136,2048]{1,0:T(8,128)(2,1)} %pack.1.refs_0_), channel_id=1, source_target_pairs={{0,1},{1,0},{2,3},{3,2},{4,5},{5,4},{6,7},{7,6},{8,9},{9,8},{10,11... | collective-permute-start | bytes 1671176 | tf_op jit(solution)/shard_map/ppermute | solution.py:358
  32.9 0.2 collective-permute-start.2
  33.1 0.3 collective-permute-start.14
  33.4 0.2 collective-permute-start.15
  33.6 7.2 %collective-permute-done.6.refs_2_ = bf16[136,2048]{1,0:T(8,128)(2,1)S(1)} collective-permute-done((bf16[136,2048]{1,0:T(8,128)(2,1)S(1)}, bf16[136,2048]{1,0:T(8,128)(2,1)S(1)}, u32[]{:S(2)}, u32[]{:S(2)}) %collective-permute-start.6) | collective-permute-done | bytes 557088 | tf_op jit(solution)/shard_map/ppermute | solution.py:368
  40.8 3.2 %collective-permute-start.12 = (bf16[136,2048]{1,0:T(8,128)(2,1)S(1)}, bf16[136,2048]{1,0:T(8,128)(2,1)S(1)}, u32[]{:S(2)}, u32[]{:S(2)}) collective-permute-start(bf16[136,2048]{1,0:T(8,128)(2,1)S(1)} %collective-permute-done.1.refs_0_), channel_id=1, source_target_pairs={{0,1},{1,0},{2,3},{3,2},{4,5},{5,4},{6,7},{7,6},{8,9},{9,8},{10,11... | collective-permute-start | bytes 1671176 | tf_op jit(solution)/shard_map/ppermute | solution.py:358
  44.0 0.7 constant_dynamic-slice_fusion
  44.9 2.2 %collective-permute-done.2.refs_0_ = bf16[136,2048]{1,0:T(8,128)(2,1)S(1)} collective-permute-done((bf16[136,2048]{1,0:T(8,128)(2,1)S(1)}, bf16[136,2048]{1,0:T(8,128)(2,1)S(1)}, u32[]{:S(2)}, u32[]{:S(2)}) %collective-permute-start.2) | collective-permute-done | bytes 557088 | tf_op jit(solution)/shard_map/ppermute | solution.py:367
  47.1 1.3 collective-permute-start.9
  48.4 0.2 collective-permute-start.8
  48.7 1.4 collective-permute-start.3
  50.2 4.6 %collective-permute-done.9.refs_5_ = bf16[72,2048]{1,0:T(8,128)(2,1)S(1)} collective-permute-done((bf16[72,2048]{1,0:T(8,128)(2,1)S(1)}, bf16[72,2048]{1,0:T(8,128)(2,1)S(1)}, u32[]{:S(2)}, u32[]{:S(2)}) %collective-permute-start.9) | collective-permute-done | bytes 294944 | tf_op jit(solution)/shard_map/ppermute | solution.py:368
  54.8 1.7 %collective-permute-start.11 = (bf16[72,2048]{1,0:T(8,128)(2,1)S(1)}, bf16[72,2048]{1,0:T(8,128)(2,1)S(1)}, u32[]{:S(2)}, u32[]{:S(2)}) collective-permute-start(bf16[72,2048]{1,0:T(8,128)(2,1)S(1)} %collective-permute-done.9.refs_5_), channel_id=1, source_target_pairs={{0,1},{1,0},{2,3},{3,2},{4,5},{5,4},{6,7},{7,6},{8,9},{9,8},{10,11... | collective-permute-start | bytes 884744 | tf_op jit(solution)/shard_map/ppermute | solution.py:358
  56.5 2.8 %copy-done = bf16[2,768,2048]{2,1,0:T(8,128)(2,1)S(1)} copy-done((bf16[2,768,2048]{2,1,0:T(8,128)(2,1)S(1)}, bf16[2,768,2048]{2,1,0:T(8,128)(2,1)}, u32[]{:S(2)}) %copy-start) | copy-done | bytes 6291480
  59.3 1.1 copy-done.3
  60.4 6.3 %shard_map.77 = (bf16[2,16,48,2048]{3,2,1,0:T(8,128)(2,1)S(1)}, bf16[16,2,48,768]{3,2,1,0:T(8,128)(2,1)}) custom-call(s32[2]{0:T(128)S(1)} %slice_bitcast_fusion.ids_ref, s32[1]{0:T(128)} %bitcast.1.me_ref, bf16[136,2048]{1,0:T(8,128)(2,1)S(1)} %copy-done.3, bf16[136,2048]{1,0:T(8,128)(2,1)} %collective-permute-done.16.refs_1_, bf16[2,768,2048]{2,1,0:T(8,128)(2,1)S(1)} %copy-done), custom_call_target="tpu_custom_call" | custom-call | flops 710934528 | bytes 8486912 | tf_op jit(solution)/shard_map/pallas_call | solution.py:202
  66.8 8.7 %shard_map.78 = (bf16[2,16,48,2048]{3,2,1,0:T(8,128)(2,1)S(1)}, bf16[16,2,48,768]{3,2,1,0:T(8,128)(2,1)}) custom-call(s32[4]{0:T(128)S(1)} %get-tuple-element.18.ids_ref, s32[1]{0:T(128)} %bitcast.1.me_ref, bf16[136,2048]{1,0:T(8,128)(2,1)S(1)} %collective-permute-done.refs_0_, ...), custom_call_target="tpu_custom_call", output_to_operand_aliasing={{0}: (7, {}), {1}: (8, {})} | custom-call | flops 1421869056 | bytes 10682368 | tf_op jit(solution)/shard_map/pallas_call | solution.py:202
  75.6 8.8 %shard_map.79 = (bf16[2,16,48,2048]{3,2,1,0:T(8,128)(2,1)S(1)}, bf16[16,2,48,768]{3,2,1,0:T(8,128)(2,1)}) custom-call(s32[4]{0:T(128)S(1)} %get-tuple-element.19.ids_ref, s32[1]{0:T(128)} %bitcast.1.me_ref, bf16[136,2048]{1,0:T(8,128)(2,1)S(1)} %collective-permute-done.1.refs_0_, ...), custom_call_target="tpu_custom_call", output_to_operand_aliasing={{0}: (7, {}), {1}: (8, {})} | custom-call | flops 1421869056 | bytes 10682368 | tf_op jit(solution)/shard_map/pallas_call | solution.py:202
  84.4 11.0 %shard_map.80 = (bf16[2,16,48,2048]{3,2,1,0:T(8,128)(2,1)S(1)}, bf16[16,2,48,768]{3,2,1,0:T(8,128)(2,1)}) custom-call(s32[6]{0:T(128)S(1)} %slice_bitcast_fusion.3.ids_ref, s32[1]{0:T(128)} %bitcast.1.me_ref, bf16[136,2048]{1,0:T(8,128)(2,1)S(1)} %collective-permute-done.2.refs_0_, ...), custom_call_target="tpu_custom_call", output_to_operand_aliasing={{0}: (11, {}), {1}: (12, {})} | custom-call | flops 2132803584 | bytes 12877824 | tf_op jit(solution)/shard_map/pallas_call | solution.py:202
  95.4 2.7 %copy-done.2 = bf16[2,16,48,2048]{3,2,1,0:T(8,128)(2,1)} copy-done((bf16[2,16,48,2048]{3,2,1,0:T(8,128)(2,1)}, bf16[2,16,48,2048]{3,2,1,0:T(8,128)(2,1)S(1)}, u32[]{:S(2)}) %copy-start.2) | copy-done | bytes 6291480
  98.0 5.4 %all-to-all-start = ((bf16[16,2,48,768]{3,2,1,0:T(8,128)(2,1)}), bf16[16,2,48,768]{3,2,1,0:T(8,128)(2,1)}, u32[]{:S(2)}, u32[]{:S(2)}) async-start(bf16[16,2,48,768]{3,2,1,0:T(8,128)(2,1)} %get-tuple-element.16), calls=%async_computation | async-start | bytes 4718592 | tf_op jit(solution)/shard_map/all_to_all | solution.py:390
  104.0 33.4 %expert_update.1 = bf16[2,768,2048]{2,1,0:T(8,128)(2,1)} custom-call(bf16[2,768,2048]{2,1,0:T(8,128)(2,1)} %bitcast.16, bf16[2,2,16,24,768]{4,3,2,1,0:T(8,128)(2,1)S(1)} %bitcast.17), custom_call_target="tpu_custom_call" | custom-call | flops 23555211264 | bytes 14942208 | tf_op jit(solution)/shard_map/expert_update/pallas_call | solution.py:313
  137.5 19.1 %all-to-all-done = bf16[16,2,48,768]{3,2,1,0:T(8,128)(2,1)} async-done(((bf16[16,2,48,768]{3,2,1,0:T(8,128)(2,1)}), bf16[16,2,48,768]{3,2,1,0:T(8,128)(2,1)}, u32[]{:S(2)}, u32[]{:S(2)}) %all-to-all-start) | async-done | bytes 2359328 | tf_op jit(solution)/shard_map/all_to_all | solution.py:390
  156.6 5.7 %fusion.2 = bf16[1024,768]{1,0:T(8,128)(2,1)} fusion(bf16[1536,768]{1,0:T(8,128)(2,1)} %bitcast.7, s32[1024]{0:T(1024)S(1)} %eq.31), kind=kOutput, calls=%fused_computation.3 | convolution fusion | flops 2418278400 | bytes 3936256 | tf_op jit(solution)/shard_map/dot_general | solution.py:400
  (38 shorter events, 1.0 us)
Async XLA Ops:
  2.6 13.7 %collective-permute-start.4 = (bf16[136,2048]{1,0:T(8,128)(2,1)}, bf16[136,2048]{1,0:T(8,128)(2,1)S(1)}, u32[]{:S(2)}, u32[]{:S(2)}) collective-permute-start(bf16[136,2048]{1,0:T(8,128)(2,1)} %pack.1.refs_0_), channel_id=1, source_target_pairs={{0,2},{1,3},{4,0},{5,1},{8,4},{9,5},{12,8},{13,9},{14,12},{15,13},... | collective-permute-start | bytes 1671176 | tf_op jit(solution)/shard_map/ppermute | solution.py:368
  3.9 13.7 %collective-permute-start = (bf16[136,2048]{1,0:T(8,128)(2,1)}, bf16[136,2048]{1,0:T(8,128)(2,1)S(1)}, u32[]{:S(2)}, u32[]{:S(2)}) collective-permute-start(bf16[136,2048]{1,0:T(8,128)(2,1)} %pack.1.refs_0_), channel_id=1, source_target_pairs={{0,4},{1,5},{4,8},{5,9},{8,12},{9,13},{12,14},{13,15},{14,10},{15,... | collective-permute-start | bytes 1671176 | tf_op jit(solution)/shard_map/ppermute | solution.py:367
  16.3 12.7 %collective-permute-start.5 = (bf16[136,2048]{1,0:T(8,128)(2,1)S(1)}, bf16[136,2048]{1,0:T(8,128)(2,1)S(1)}, u32[]{:S(2)}, u32[]{:S(2)}) collective-permute-start(bf16[136,2048]{1,0:T(8,128)(2,1)S(1)} %collective-permute-done.4.refs_2_), channel_id=1, source_target_pairs={{0,2},{1,3},{4,0},{5,1},{8,4},{9,5},{12,8},{13,9},{14,12},{15,13},... | collective-permute-start | bytes 1671176 | tf_op jit(solution)/shard_map/ppermute | solution.py:368
  17.6 15.3 %collective-permute-start.1 = (bf16[136,2048]{1,0:T(8,128)(2,1)S(1)}, bf16[136,2048]{1,0:T(8,128)(2,1)S(1)}, u32[]{:S(2)}, u32[]{:S(2)}) collective-permute-start(bf16[136,2048]{1,0:T(8,128)(2,1)S(1)} %collective-permute-done.refs_0_), channel_id=1, source_target_pairs={{0,4},{1,5},{4,8},{5,9},{8,12},{9,13},{12,14},{13,15},{14,10},{15,... | collective-permute-start | bytes 1671176 | tf_op jit(solution)/shard_map/ppermute | solution.py:367
  29.0 11.8 %collective-permute-start.6 = (bf16[136,2048]{1,0:T(8,128)(2,1)S(1)}, bf16[136,2048]{1,0:T(8,128)(2,1)S(1)}, u32[]{:S(2)}, u32[]{:S(2)}) collective-permute-start(bf16[136,2048]{1,0:T(8,128)(2,1)S(1)} %collective-permute-done.5.refs_2_), channel_id=1, source_target_pairs={{0,2},{1,3},{4,0},{5,1},{8,4},{9,5},{12,8},{13,9},{14,12},{15,13},... | collective-permute-start | bytes 1671176 | tf_op jit(solution)/shard_map/ppermute | solution.py:368
  30.3 14.5 %collective-permute-start.16 = (bf16[136,2048]{1,0:T(8,128)(2,1)}, bf16[136,2048]{1,0:T(8,128)(2,1)}, u32[]{:S(2)}, u32[]{:S(2)}) collective-permute-start(bf16[136,2048]{1,0:T(8,128)(2,1)} %pack.1.refs_0_), channel_id=1, source_target_pairs={{0,1},{1,0},{2,3},{3,2},{4,5},{5,4},{6,7},{7,6},{8,9},{9,8},{10,11... | collective-permute-start | bytes 1671176 | tf_op jit(solution)/shard_map/ppermute | solution.py:358
  32.9 14.2 %collective-permute-start.2 = (bf16[136,2048]{1,0:T(8,128)(2,1)S(1)}, bf16[136,2048]{1,0:T(8,128)(2,1)S(1)}, u32[]{:S(2)}, u32[]{:S(2)}) collective-permute-start(bf16[136,2048]{1,0:T(8,128)(2,1)S(1)} %collective-permute-done.1.refs_0_), channel_id=1, source_target_pairs={{0,4},{1,5},{4,8},{5,9},{8,12},{9,13},{12,14},{13,15},{14,10},{15,... | collective-permute-start | bytes 1671176 | tf_op jit(solution)/shard_map/ppermute | solution.py:367
  33.1 15.3 %collective-permute-start.14 = (bf16[136,2048]{1,0:T(8,128)(2,1)S(1)}, bf16[136,2048]{1,0:T(8,128)(2,1)S(1)}, u32[]{:S(2)}, u32[]{:S(2)}) collective-permute-start(bf16[136,2048]{1,0:T(8,128)(2,1)S(1)} %collective-permute-done.refs_0_), channel_id=1, source_target_pairs={{0,1},{1,0},{2,3},{3,2},{4,5},{5,4},{6,7},{7,6},{8,9},{9,8},{10,11... | collective-permute-start | bytes 1671176 | tf_op jit(solution)/shard_map/ppermute | solution.py:358
  33.4 15.3 %collective-permute-start.15 = (bf16[136,2048]{1,0:T(8,128)(2,1)S(1)}, bf16[136,2048]{1,0:T(8,128)(2,1)S(1)}, u32[]{:S(2)}, u32[]{:S(2)}) collective-permute-start(bf16[136,2048]{1,0:T(8,128)(2,1)S(1)} %collective-permute-done.4.refs_2_), channel_id=1, source_target_pairs={{0,1},{1,0},{2,3},{3,2},{4,5},{5,4},{6,7},{7,6},{8,9},{9,8},{10,11... | collective-permute-start | bytes 1671176 | tf_op jit(solution)/shard_map/ppermute | solution.py:358
  40.8 9.3 %collective-permute-start.12 = (bf16[136,2048]{1,0:T(8,128)(2,1)S(1)}, bf16[136,2048]{1,0:T(8,128)(2,1)S(1)}, u32[]{:S(2)}, u32[]{:S(2)}) collective-permute-start(bf16[136,2048]{1,0:T(8,128)(2,1)S(1)} %collective-permute-done.1.refs_0_), channel_id=1, source_target_pairs={{0,1},{1,0},{2,3},{3,2},{4,5},{5,4},{6,7},{7,6},{8,9},{9,8},{10,11... | collective-permute-start | bytes 1671176 | tf_op jit(solution)/shard_map/ppermute | solution.py:358
  44.8 30.7 %collective-permute-start.13 = (bf16[136,2048]{1,0:T(8,128)(2,1)S(1)}, bf16[136,2048]{1,0:T(8,128)(2,1)S(1)}, u32[]{:S(2)}, u32[]{:S(2)}) collective-permute-start(bf16[136,2048]{1,0:T(8,128)(2,1)S(1)} %collective-permute-done.5.refs_2_), channel_id=1, source_target_pairs={{0,1},{1,0},{2,3},{3,2},{4,5},{5,4},{6,7},{7,6},{8,9},{9,8},{10,11... | collective-permute-start | bytes 1671176 | tf_op jit(solution)/shard_map/ppermute | solution.py:358
  47.1 7.7 %collective-permute-start.9 = (bf16[72,2048]{1,0:T(8,128)(2,1)S(1)}, bf16[72,2048]{1,0:T(8,128)(2,1)S(1)}, u32[]{:S(2)}, u32[]{:S(2)}) collective-permute-start(bf16[72,2048]{1,0:T(8,128)(2,1)S(1)} %slice.41), channel_id=1, source_target_pairs={{0,2},{1,3},{4,0},{5,1},{8,4},{9,5},{12,8},{13,9},{14,12},{15,13},... | collective-permute-start | bytes 884744 | tf_op jit(solution)/shard_map/ppermute | solution.py:368
  48.4 18.3 %collective-permute-start.8 = (bf16[64,2048]{1,0:T(8,128)(2,1)S(1)}, bf16[64,2048]{1,0:T(8,128)(2,1)S(1)}, u32[]{:S(2)}, u32[]{:S(2)}) collective-permute-start(bf16[64,2048]{1,0:T(8,128)(2,1)S(1)} %slice.40), channel_id=1, source_target_pairs={{0,4},{1,5},{4,8},{5,9},{8,12},{9,13},{12,14},{13,15},{14,10},{15,... | collective-permute-start | bytes 786440 | tf_op jit(solution)/shard_map/ppermute | solution.py:367
  48.7 35.7 %collective-permute-start.3 = (bf16[136,2048]{1,0:T(8,128)(2,1)S(1)}, bf16[136,2048]{1,0:T(8,128)(2,1)S(1)}, u32[]{:S(2)}, u32[]{:S(2)}) collective-permute-start(bf16[136,2048]{1,0:T(8,128)(2,1)S(1)} %collective-permute-done.2.refs_0_), channel_id=1, source_target_pairs={{0,1},{1,0},{2,3},{3,2},{4,5},{5,4},{6,7},{7,6},{8,9},{9,8},{10,11... | collective-permute-start | bytes 1671176 | tf_op jit(solution)/shard_map/ppermute | solution.py:358
  50.1 34.3 %collective-permute-start.7 = (bf16[136,2048]{1,0:T(8,128)(2,1)S(1)}, bf16[136,2048]{1,0:T(8,128)(2,1)S(1)}, u32[]{:S(2)}, u32[]{:S(2)}) collective-permute-start(bf16[136,2048]{1,0:T(8,128)(2,1)S(1)} %collective-permute-done.6.refs_2_), channel_id=1, source_target_pairs={{0,1},{1,0},{2,3},{3,2},{4,5},{5,4},{6,7},{7,6},{8,9},{9,8},{10,11... | collective-permute-start | bytes 1671176 | tf_op jit(solution)/shard_map/ppermute | solution.py:358
  54.8 29.6 %collective-permute-start.11 = (bf16[72,2048]{1,0:T(8,128)(2,1)S(1)}, bf16[72,2048]{1,0:T(8,128)(2,1)S(1)}, u32[]{:S(2)}, u32[]{:S(2)}) collective-permute-start(bf16[72,2048]{1,0:T(8,128)(2,1)S(1)} %collective-permute-done.9.refs_5_), channel_id=1, source_target_pairs={{0,1},{1,0},{2,3},{3,2},{4,5},{5,4},{6,7},{7,6},{8,9},{9,8},{10,11... | collective-permute-start | bytes 884744 | tf_op jit(solution)/shard_map/ppermute | solution.py:358
  56.5 2.8 %copy-start = (bf16[2,768,2048]{2,1,0:T(8,128)(2,1)S(1)}, bf16[2,768,2048]{2,1,0:T(8,128)(2,1)}, u32[]{:S(2)}) copy-start(bf16[2,768,2048]{2,1,0:T(8,128)(2,1)} %refs_8_.1) | copy-start | bytes 18874372
  59.3 1.1 copy-start.3
  60.4 6.4 %copy-start.1 = (bf16[2,768,2048]{2,1,0:T(8,128)(2,1)S(1)}, bf16[2,768,2048]{2,1,0:T(8,128)(2,1)}, u32[]{:S(2)}) copy-start(bf16[2,768,2048]{2,1,0:T(8,128)(2,1)} %refs_8_.1) | copy-start | bytes 18874372
  66.7 17.6 %collective-permute-start.10 = (bf16[64,2048]{1,0:T(8,128)(2,1)S(1)}, bf16[64,2048]{1,0:T(8,128)(2,1)S(1)}, u32[]{:S(2)}, u32[]{:S(2)}) collective-permute-start(bf16[64,2048]{1,0:T(8,128)(2,1)S(1)} %collective-permute-done.8.refs_4_), channel_id=1, source_target_pairs={{0,1},{1,0},{2,3},{3,2},{4,5},{5,4},{6,7},{7,6},{8,9},{9,8},{10,11... | collective-permute-start | bytes 786440 | tf_op jit(solution)/shard_map/ppermute | solution.py:358
  95.3 2.7 %copy-start.2 = (bf16[2,16,48,2048]{3,2,1,0:T(8,128)(2,1)}, bf16[2,16,48,2048]{3,2,1,0:T(8,128)(2,1)S(1)}, u32[]{:S(2)}) copy-start(bf16[2,16,48,2048]{3,2,1,0:T(8,128)(2,1)S(1)} %get-tuple-element.17) | copy-start | bytes 18874372
  98.0 5.4 %copy-start.5 = (s32[2,64,8]{1,2,0:T(8,128)S(1)}, s32[2,64,8]{1,2,0:T(8,128)}, u32[]{:S(2)}) copy-start(s32[2,64,8]{1,2,0:T(8,128)} %param.6) | copy-start | bytes 12292
  98.0 6.0 %copy-start.4 = (bf16[2,2,384,768]{3,2,1,0:T(8,128)(2,1)S(1)}, bf16[2,2,384,768]{3,2,1,0:T(8,128)(2,1)}, u32[]{:S(2)}) copy-start(bf16[2,2,384,768]{3,2,1,0:T(8,128)(2,1)} %param.9) | copy-start | bytes 7077892
  98.0 58.5 %all-to-all-start = ((bf16[16,2,48,768]{3,2,1,0:T(8,128)(2,1)}), bf16[16,2,48,768]{3,2,1,0:T(8,128)(2,1)}, u32[]{:S(2)}, u32[]{:S(2)}) async-start(bf16[16,2,48,768]{3,2,1,0:T(8,128)(2,1)} %get-tuple-element.16), calls=%async_computation | async-start | bytes 4718592 | tf_op jit(solution)/shard_map/all_to_all | solution.py:390
